TPU v7x, 128 devices: a whole 4x4x4 slice. The times are simulated.
128 devices in a mesh: outer: 16 (over y, x), inner: 8 (over z, core).
Axes of the slice: x: 4, y: 4, z: 4, core: 2. Of those that a mesh axis runs over, the one named last changes fastest.
Arguments:
- world_shocks: float32 [256, 2, 128], P('outer'), may hold values from -6 to 6
- short_rate: float32 [256, 2], P('outer'), may hold values from 0 to 0.06
- inner_shocks: float32 [2, 128, 16384], P(None, 'outer', 'inner'), may hold values from -12 to 12
- fund_volatility: float32 [128], P('outer'), may hold values from 0.08 to 0.25
- fund_index: int32 [256, 4], P('outer'), may hold values from 0 to 127
- allocation: float32 [256, 4], P('outer'), may hold values from 0.1 to 1
- guarantee_type: int32 [256], P('outer'), may hold values from 0 to 1
- maturity: int32 [256], P('outer'), may hold values from 1 to 64
- guarantee_ratio: float32 [256], P('outer'), may hold values from 0.7 to 1.4
- fee_rate: float32 [256], P('outer'), may hold values from 0.005 to 0.03
- mortality: float32 [256], P('outer'), may hold values from 0.004 to 0.05
- account: float32 [256], P('outer'), may hold values from 1 to 8
Outputs:
- reserve: float32 [256, 2, 256], P(('outer', 'inner'))
- reserve_rho: float32 [256, 2, 256], P(('outer', 'inner'))
- fund_delta: float32 [256, 2, 128], P(('outer', 'inner'))
All inputs are finite; a program needn't handle non-finite values.
Results may differ from a plain program's by a relative error of at most 0.0025.
Values may be sent and summed in bfloat16 or wider, within the bound.
A program may use at most 64 MiB of HBM per device.

v0:
```python
import functools
import math

import jax
import jax.numpy as jnp
from jax import lax
from jax.experimental import pallas as pl
from jax.experimental.pallas import tpu as pltpu
from jax.sharding import PartitionSpec as P

MESH = pl.DeviceIdType.MESH
HIGHEST = lax.Precision.HIGHEST
F32, BF16 = jnp.float32, jnp.bfloat16

STEPS = 64
DRIFT = 0.06
SMOOTH = 0.05
NOUT = 16
NIN = 8
TILES = 32
GROUPS = 16
TYPE, MAT, RATIO, FEE, MORT, ACC, SIG, KEY = 8, 9, 10, 11, 12, 13, 14, 15
SLAB = 24
LOG2E = 1.0 / math.log(2.0)
UNIT = LOG2E / SMOOTH


def dot(a, b, dims=((1,), (0,)), precision=None):
    return lax.dot_general(
        a, b, (dims, ((), ())), precision=precision, preferred_element_type=F32
    )


def dot01(a, b, dims=((1,), (0,)), parts=3):
    b = b.astype(BF16)
    total = None
    for _ in range(parts):
        top = a.astype(BF16)
        a = a - top.astype(F32)
        one = dot(top, b, dims)
        total = one if total is None else total + one
    return total


def iota(shape, dim):
    return lax.broadcasted_iota(jnp.int32, shape, dim)


def factor_kernel(
    me,
    shocks_ref,
    sigma_ref,
    index_ref,
    alloc_ref,
    kind_ref,
    mat_ref,
    ratio_ref,
    fee_ref,
    mort_ref,
    acc_ref,
    out_ref,
    table_ref,
    scratch,
):
    me = lax.axis_index("outer") if me is None else me
    sigma_row = sigma_ref[...]
    mat = mat_ref[...].astype(F32)
    number = (iota((1, 16), 1) + 16 * me).astype(F32)
    key = jnp.where(kind_ref[...] == 0, 128.0 - mat, 256.0 + mat) * 256.0 + number
    scratch[...] = jnp.zeros((16, 128), F32)
    scratch[0:4, 0:16] = index_ref[...].astype(F32)
    scratch[4:8, 0:16] = alloc_ref[...]
    scratch[TYPE : TYPE + 1, 0:16] = kind_ref[...].astype(F32)
    scratch[MAT : MAT + 1, 0:16] = mat
    scratch[RATIO : RATIO + 1, 0:16] = ratio_ref[...]
    scratch[FEE : FEE + 1, 0:16] = fee_ref[...]
    scratch[MORT : MORT + 1, 0:16] = mort_ref[...]
    scratch[ACC : ACC + 1, 0:16] = acc_ref[...]
    scratch[SIG : SIG + 1, 0:8] = sigma_row
    scratch[KEY : KEY + 1, 0:16] = key
    table_ref[...] = pltpu.roll(scratch[...], 16 * lax.rem(me, 8), 1)

    rows = jnp.concatenate(
        [shocks_ref[m, :, 128 * j : 128 * j + 128] for m in range(2) for j in range(16)],
        axis=0,
    )
    src, dst = iota((128, 128), 0), iota((128, 128), 1)
    upper = (src // 64 == dst // 64) & (src <= dst)
    running = dot01(rows, upper.astype(F32))
    same = iota((8, 8), 0) == iota((8, 8), 1)
    sigma = jnp.sum(jnp.where(same, sigma_row, 0.0), axis=1, keepdims=True)
    sigma = jnp.broadcast_to(sigma[None], (32, 8, 1)).reshape(256, 1)
    horizon = (iota((1, 128), 1) % 64 + 1).astype(F32)
    factor = jnp.exp(-0.5 * sigma * sigma * horizon + sigma * running)
    lane = iota((8, 128), 1)
    months = []
    for m in range(2):
        regs = [factor[(m * 16 + j) * 8 : (m * 16 + j) * 8 + 8] for j in range(16)]
        for bit in range(4):
            low = (lane // (4 << bit)) % 2 == 0
            step = 4 << bit
            fresh = list(regs)
            for j in range(16):
                if j >> bit & 1:
                    continue
                k = j | 1 << bit
                a, b = regs[j], regs[k]
                fresh[j] = jnp.where(low, a, pltpu.roll(b, step, 1))
                fresh[k] = jnp.where(low, pltpu.roll(a, 128 - step, 1), b)
            regs = fresh
        months.append(regs)
    for g in range(16):
        both = jnp.concatenate([months[0][g], months[1][g]], axis=0)
        out_ref[:, 128 * g : 128 * g + 128] = both.astype(BF16)


def own_factor(shocks, sigma, index, alloc, *rest, me=None):
    return pl.pallas_call(
        functools.partial(factor_kernel, me),
        out_shape=(
            jax.ShapeDtypeStruct((16, 2048), BF16),
            jax.ShapeDtypeStruct((16, 128), F32),
        ),
        scratch_shapes=[pltpu.VMEM((16, 128), F32)],
        name="own_factor",
    )(shocks, sigma[None], index.T, alloc.T, *(value[None] for value in rest))


def gather_kernel(block_ref, table_ref, blocks_ref, tables_ref, send, recv, own):
    me = lax.axis_index("outer")
    barrier = pltpu.get_barrier_semaphore()
    for d in range(1, NOUT):
        pl.semaphore_signal(
            barrier, inc=1, device_id={"outer": lax.rem(me + d, NOUT)}, device_id_type=MESH
        )
    pl.semaphore_wait(barrier, NOUT - 1)
    copies = []
    for d in range(1, NOUT):
        peer = lax.rem(me + d, NOUT)
        for n, (src, dst) in enumerate(((table_ref, tables_ref), (block_ref, blocks_ref))):
            copy = pltpu.make_async_remote_copy(
                src_ref=src,
                dst_ref=dst.at[me],
                send_sem=send.at[n, d],
                recv_sem=recv.at[n, d],
                device_id={"outer": peer},
                device_id_type=MESH,
            )
            copy.start()
            copies.append(copy)
    mine = [
        pltpu.make_async_copy(table_ref, tables_ref.at[me], own.at[0]),
        pltpu.make_async_copy(block_ref, blocks_ref.at[me], own.at[1]),
    ]
    for copy in mine:
        copy.start()
    for copy in mine:
        copy.wait()
    for copy in copies:
        copy.wait()


def gather_outer(block, table):
    vmem = pl.BlockSpec(memory_space=pltpu.VMEM)
    anywhere = pl.BlockSpec(memory_space=pl.ANY)
    return pl.pallas_call(
        gather_kernel,
        out_shape=(
            jax.ShapeDtypeStruct((NOUT, 16, 2048), BF16),
            jax.ShapeDtypeStruct((NOUT, 16, 128), F32),
        ),
        in_specs=[vmem, vmem],
        out_specs=(anywhere, anywhere),
        scratch_shapes=[
            pltpu.SemaphoreType.DMA((2, NOUT)),
            pltpu.SemaphoreType.DMA((2, NOUT)),
            pltpu.SemaphoreType.DMA((2,)),
        ],
        compiler_params=pltpu.CompilerParams(collective_id=0, has_side_effects=True),
        name="gather_outer",
    )(block, table)


def value_kernel(
    blocks_ref,
    tables_ref,
    world_ref,
    rate_ref,
    out_ref,
    fmat,
    fmat_t,
    level,
    weight_t,
    dwt,
    rows_t,
    acc_t,
    table,
    plan_v,
    plan,
    sums_t,
    sens,
    sums_in,
    kerns,
    sem,
):
    params_t = jnp.concatenate(
        [sum(tables_ref[s] for s in range(8)), sum(tables_ref[s] for s in range(8, 16))],
        axis=1,
    )
    params = params_t.T
    key_col, key_row = params[:, KEY : KEY + 1], params_t[KEY : KEY + 1]
    rank_col = jnp.sum((key_row < key_col).astype(F32), axis=1, keepdims=True)
    rank_row = jnp.sum((key_col < key_row).astype(F32), axis=0, keepdims=True)
    place = (rank_col == iota((256, 256), 1).astype(F32)).astype(F32)
    ordered = dot01(params_t, place)
    table[0] = ordered[:, :128]
    table[1] = ordered[:, 128:]

    mat = ordered[MAT : MAT + 1]
    first = jnp.where(ordered[TYPE : TYPE + 1] == 0.0, 1.0, mat)
    tile_of = iota((TILES, 256), 1) // 8 == iota((TILES, 256), 0)
    low = jnp.min(jnp.where(tile_of, first, 1e3), axis=1, keepdims=True)
    high = jnp.max(jnp.where(tile_of, mat, 0.0), axis=1, keepdims=True)
    low = jnp.floor((low - 1.0) * 0.25)
    count = jnp.floor((jnp.floor((high - 1.0) * 0.25) - low) * 0.5) + 1.0
    before = (iota((TILES, TILES), 1) < iota((TILES, TILES), 0)).astype(F32)
    begin = dot(before, jnp.broadcast_to(count, (TILES, 384)))
    item = iota((TILES, 384), 1).astype(F32)
    mine = (begin <= item) & (item < begin + count)
    tile_id = iota((TILES, 384), 0).astype(F32)
    plan_v[0:1, :] = jnp.sum(jnp.where(mine, tile_id, 0.0), axis=0, keepdims=True).astype(jnp.int32)
    place_g = jnp.where(mine, low + 2.0 * (item - begin), 0.0)
    plan_v[1:2, :] = jnp.sum(place_g, axis=0, keepdims=True).astype(jnp.int32)
    items = jnp.sum(mine.astype(F32), axis=(0, 1), keepdims=True)
    plan_v[2:8, :] = jnp.broadcast_to(items, (6, 384)).astype(jnp.int32)
    copy = pltpu.make_async_copy(plan_v, plan, sem)
    copy.start()

    spread_o = (iota((16, 128), 1) % 16 == iota((16, 128), 0)).astype(F32)
    sigma = params[:, SIG : SIG + 1].reshape(16, 2, 8, 1)[:, 0].reshape(128, 1)
    total = jnp.zeros((128, 128), F32)
    rates = []
    rate_col = rate_ref[...].T
    for m in range(2):
        shock = dot01(world_ref[:, m, :], spread_o, ((0,), (0,)))
        total = total + (
            (DRIFT - 0.5 * sigma * sigma) / 12.0 + sigma * shock / math.sqrt(12.0)
        )
        level[m] = jnp.exp(total)
        rate = jnp.sum(rate_col[:, m : m + 1] * spread_o, axis=0, keepdims=True)
        rates.append(jnp.broadcast_to(rate, (8, 128)))

    fund = iota((128, 128), 0).astype(F32)
    step_in = iota((8, 128), 0) % 4

    def build(j, carry):
        where = 8 * lax.rem(j, 16) + iota((16, 128), 1) // 16
        rows = jnp.take_along_axis(table[j // 16], where, axis=1)

        def row(k):
            return rows[k : k + 1]

        share_sum = row(4) + row(5) + row(6) + row(7)
        wts = jnp.zeros((128, 128), F32)
        for k in range(4):
            wts = wts + jnp.where(fund == row(k), row(4 + k) / share_sum, 0.0)
        dwt[j] = wts * row(ACC)
        zero = jnp.zeros((16, 8, 128), F32)
        for m in range(2):
            one = (wts * level[m]).reshape(16, 8, 128)
            both = [one, zero] if m == 0 else [zero, one]
            both = jnp.stack(both, axis=1).reshape(256, 128)
            weight_t[j, :, 128 * m : 128 * m + 128] = both.astype(BF16)
            sens[j, m] = jnp.zeros((128, 128), F32)
        for n in range(4):
            sums_t[j, n] = jnp.zeros((8, 128), F32)
        death = row(TYPE) == 0.0
        mat = row(MAT)
        log_keep = jnp.log(1.0 - row(MORT))
        rows_t[j, 0:1] = jnp.where(death, 1.0, mat)
        rows_t[j, 1:2] = mat
        rows_t[j, 2:3] = jnp.where(death, row(MORT), 1.0)
        rows_t[j, 3:4] = jnp.where(death, log_keep, 0.0) * LOG2E
        rows_t[j, 4:5] = jnp.where(death, -log_keep, log_keep * mat) * LOG2E
        rows_t[j, 5:6] = row(FEE) * LOG2E
        rows_t[j, 6:7] = row(RATIO) * UNIT
        acc_t[pl.ds(j, 1), :] = row(ACC)
        return carry

    lax.fori_loop(0, TILES, build, 0)

    for g in range(GROUPS):
        cols = slice(128 * g, 128 * g + 128)
        part = blocks_ref[:, :, cols].astype(F32).reshape(16, 2, 8, 128)
        for m in range(2):
            one = part[:, m].reshape(128, 128)
            fmat[m, :, cols] = one.astype(BF16)
        fmat_t[cols, :] = part.reshape(256, 128).T.astype(BF16)
    fmat[:, :, 2048:] = jnp.zeros((2, 128, 128), BF16)
    fmat_t[2048:, :] = jnp.zeros((256, 256), BF16)
    copy.wait()

    def raw(j, g):
        here = pl.ds(pl.multiple_of(g * 128, 128), 128)
        return dot(fmat_t[here, :], weight_t[j])

    rates2 = [rate * LOG2E for rate in rates]

    def group(j, g, slot):
        def wide(k):
            return jnp.broadcast_to(rows_t[j, k : k + 1], (8, 128))

        hz = (step_in + (4 * g + 1)).astype(F32)
        fee = wide(5)
        decay = jnp.where(
            (hz >= wide(0)) & (hz <= wide(1)),
            wide(2) * lax.exp2(wide(3) * hz + wide(4)),
            0.0,
        )
        fee_decay = lax.exp2(-fee * hz) * decay
        strike = wide(6)
        for m in range(2):
            growth = lax.exp2((rates2[m] - fee) * hz) * UNIT
            weight = decay * lax.exp2(-rates2[m] * hz)
            y = sums_in[slot, :, 128 * m : 128 * m + 128].reshape(16, 8, 128) * growth
            x = strike - y
            up = lax.exp2(x)
            more = 1.0 + up
            soft = jnp.where(up < 2.0**-12, up, jnp.log(more))
            slope = up / more
            kern = (fee_decay * slope).reshape(128, 128).astype(BF16)
            soft_sum = jnp.sum(soft, axis=0)
            rho_sum = soft_sum + jnp.sum(slope * y, axis=0) * (1.0 / LOG2E)
            sums_t[j, 2 * m] += weight * soft_sum
            sums_t[j, 2 * m + 1] += (hz * weight) * rho_sum
            kerns[m, 128 * slot : 128 * slot + 128, :] = kern

    def flush(j, g):
        here = pl.ds(pl.multiple_of(g * 128, 128), 256)
        for m in range(2):
            sens[j, m] += dot(fmat[m, :, here], kerns[m])

    total = plan[2, 0]
    kerns[...] = jnp.zeros((2, 256, 128), BF16)
    sums_in[0] = raw(plan[0, 0], plan[1, 0])

    def work(i, carry):
        j, g = plan[0, i], plan[1, i]
        last = jnp.maximum(i - 1, 0)
        flush(plan[0, last], plan[1, last])
        sums_in[1] = raw(j, g + 1)
        group(j, g, 0)
        sums_in[0] = raw(plan[0, i + 1], plan[1, i + 1])
        group(j, g + 1, 1)
        return carry

    lax.fori_loop(0, total, work, 0)
    flush(plan[0, total - 1], plan[1, total - 1])

    def close(q, deltas):
        fresh = list(deltas)
        for k in range(4):
            j = 4 * q + k
            for m in range(2):
                fresh[m] = fresh[m] + dwt[j] * sens[j, m]
        return tuple(fresh)

    none = jnp.zeros((128, 128), F32)
    delta = lax.fori_loop(0, TILES // 4, close, (none, none))
    scale = acc_t[...] * (1.0 / 20.0 / 256.0)
    res_acc = []
    for n in range(4):
        value = jnp.sum(sums_t[:, n], axis=1)
        res_acc.append(value * (scale if n % 2 == 0 else -scale))

    tile_row = jnp.floor(rank_row * 0.125)
    slot_row = rank_row - 8.0 * tile_row
    pick = (tile_row == iota((TILES, 256), 0).astype(F32)).astype(F32)
    keep = (slot_row == (iota((128, 256), 0) // 16).astype(F32)).astype(F32)
    for m in range(2):
        parts = []
        for n in range(2):
            lanes = dot01(res_acc[2 * m + n], pick, ((0,), (0,)))
            parts.append(jnp.sum((lanes * keep).reshape(8, 16, 256), axis=0))
        down = delta[m].T.reshape(8, 16, 128)
        parts.append(jnp.sum(down, axis=0) * (-1.0 / 256.0))
        line = jnp.concatenate(parts, axis=1)
        for o in range(16):
            for k in range(5):
                r = (o % 2) * 10 + m * 5 + k
                out_ref[o // 2, r : r + 1, :] = line[o : o + 1, 128 * k : 128 * k + 128]
    for b in range(NIN):
        out_ref[b, 20:SLAB, :] = jnp.zeros((SLAB - 20, 128), F32)


def revalue(blocks, tables, world, rate):
    return pl.pallas_call(
        value_kernel,
        out_shape=jax.ShapeDtypeStruct((NIN, SLAB, 128), F32),
        scratch_shapes=[
            pltpu.VMEM((2, 128, 2176), BF16),
            pltpu.VMEM((2304, 256), BF16),
            pltpu.VMEM((2, 128, 128), F32),
            pltpu.VMEM((TILES, 256, 256), BF16),
            pltpu.VMEM((TILES, 128, 128), F32),
            pltpu.VMEM((TILES, 8, 128), F32),
            pltpu.VMEM((TILES, 128), F32),
            pltpu.VMEM((2, 16, 128), F32),
            pltpu.VMEM((8, 384), jnp.int32),
            pltpu.SMEM((8, 384), jnp.int32),
            pltpu.VMEM((TILES, 4, 8, 128), F32),
            pltpu.VMEM((TILES, 2, 128, 128), F32),
            pltpu.VMEM((2, 128, 256), F32),
            pltpu.VMEM((2, 256, 128), BF16),
            pltpu.SemaphoreType.DMA(()),
        ],
        name="revalue",
    )(blocks, tables, world, rate.T)


def scatter_kernel(slabs_ref, out_ref, inbox, send, recv):
    me = lax.axis_index("inner")
    barrier = pltpu.get_barrier_semaphore()
    for d in range(1, NIN):
        pl.semaphore_signal(
            barrier, inc=1, device_id={"inner": lax.rem(me + d, NIN)}, device_id_type=MESH
        )
    pl.semaphore_wait(barrier, NIN - 1)
    copies = []
    for d in range(1, NIN):
        peer = lax.rem(me + d, NIN)
        copy = pltpu.make_async_remote_copy(
            src_ref=slabs_ref.at[peer],
            dst_ref=inbox.at[d],
            send_sem=send.at[d],
            recv_sem=recv.at[d],
            device_id={"inner": peer},
            device_id_type=MESH,
        )
        copy.start()
        copies.append(copy)
    total = slabs_ref[me]
    for d in range(1, NIN):
        copies[d - 1].wait()
        total = total + inbox[d]
    out_ref[...] = total


def scatter_inner(slabs):
    vmem = pl.BlockSpec(memory_space=pltpu.VMEM)
    return pl.pallas_call(
        scatter_kernel,
        out_shape=jax.ShapeDtypeStruct((SLAB, 128), F32),
        in_specs=[vmem],
        out_specs=vmem,
        scratch_shapes=[
            pltpu.VMEM((NIN, SLAB, 128), F32),
            pltpu.SemaphoreType.DMA((NIN,)),
            pltpu.SemaphoreType.DMA((NIN,)),
        ],
        compiler_params=pltpu.CompilerParams(collective_id=1, has_side_effects=True),
        name="scatter_inner",
    )(slabs)


def shards(
    world_shocks,
    short_rate,
    inner_shocks,
    fund_volatility,
    fund_index,
    allocation,
    guarantee_type,
    maturity,
    guarantee_ratio,
    fee_rate,
    mortality,
    account,
):
    block, table = own_factor(
        inner_shocks,
        fund_volatility,
        fund_index,
        allocation,
        guarantee_type,
        maturity,
        guarantee_ratio,
        fee_rate,
        mortality,
        account,
    )
    blocks, tables = gather_outer(block, table)
    slabs = revalue(blocks, tables, world_shocks, short_rate)
    total = scatter_inner(slabs)[:20].reshape(2, 2, 5 * 128)
    return total[..., :256], total[..., 256:512], total[..., 512:]


def solution(mesh):
    return jax.shard_map(
        shards,
        mesh=mesh,
        in_specs=(
            P("outer", None, None),
            P("outer", None),
            P(None, "outer", "inner"),
            P("outer"),
            P("outer", None),
            P("outer", None),
            P("outer"),
            P("outer"),
            P("outer"),
            P("outer"),
            P("outer"),
            P("outer"),
        ),
        out_specs=(
            P(("outer", "inner"), None, None),
            P(("outer", "inner"), None, None),
            P(("outer", "inner"), None, None),
        ),
        check_vma=False,
    )
```

profile of v0, /device:TPU:1, one launch (start us, length us, event | category | flops | bytes accessed | tf_op | source)
XLA Modules:
  0.0 76.4 jit_solution(4262314338532515179)
XLA Ops:
  0.6 2.1 %own_factor.1 = (bf16[16,2048]{1,0:T(8,128)(2,1)}, f32[16,128]{1,0:T(8,128)}) custom-call(f32[2,8,2048]{2,1,0:T(8,128)} %shocks_ref.1, f32[1,8]{1,0:T(1,128)} %bitcast.15, s32[4,16]{1,0:T(4,128)} %bitcast.12, f32[4,16]{1,0:T(4,128)} %bitcast.13, s32[1,16]{1,0:T(1,128)} %bitcast.16, s32[1,16]{1,0:T(1,128)} %bitcast.17, f32[1,16]{1,0:T(1,128)} %bitcast.18, ...), custom_call_target="tpu_custom_call" | custom-call | tf_op jit(solution)/shard_map/own_factor/pallas_call | solution.py:118
  2.7 22.8 %gather_outer.1 = (bf16[16,16,2048]{2,1,0:T(8,128)(2,1)}, f32[16,16,128]{2,1,0:T(8,128)}) custom-call(bf16[16,2048]{1,0:T(8,128)(2,1)} %get-tuple-element.7.block_ref, f32[16,128]{1,0:T(8,128)} %get-tuple-element.8.table_ref), custom_call_target="tpu_custom_call" | custom-call | tf_op jit(solution)/shard_map/gather_outer/pallas_call | solution.py:166
  25.6 38.5 %revalue.1.slabs_ref = f32[8,24,128]{2,1,0:T(8,128)} custom-call(bf16[16,16,2048]{2,1,0:T(8,128)(2,1)} %get-tuple-element.9.blocks_ref, f32[16,16,128]{2,1,0:T(8,128)} %get-tuple-element.10.tables_ref, f32[16,2,128]{2,1,0:T(2,128)} %world_ref.1, f32[2,16]{1,0:T(2,128)} %bitcast.14), custom_call_target="tpu_custom_call" | custom-call | tf_op jit(solution)/shard_map/revalue/pallas_call | solution.py:397
  64.1 10.4 %scatter_inner.1 = f32[24,128]{1,0:T(8,128)} custom-call(f32[8,24,128]{2,1,0:T(8,128)} %revalue.1.slabs_ref), custom_call_target="tpu_custom_call" | custom-call | tf_op jit(solution)/shard_map/scatter_inner/pallas_call | solution.py:451
  74.5 0.7 reshape.9
  75.2 0.6 slice.18
  75.8 0.6 fusion
where the time goes:
time: 75.1 us; the launch traced here: 76.4 us
  Pallas kernels  73.8 us (98%)
  local copies, waits for them, and re-layouts  1.9 us (3%)
    pallas_call x1, Pallas kernels, revalue(): pl.pallas_call(value_kernel, out_shape=jax.ShapeDtypeStruct((NIN, SLAB, 1...  38.5 us
    pallas_call x1, Pallas kernels, gather_outer(): pl.pallas_call(gather_kernel, out_shape=(jax.ShapeDtypeStruct((NOUT, 16,...  22.8 us
    pallas_call x1, Pallas kernels, scatter_inner(): pl.pallas_call(scatter_kernel, out_shape=jax.ShapeDtypeStruct((SLAB, 128)...  10.4 us
    pallas_call x1, Pallas kernels, own_factor(): pl.pallas_call(functools.partial(factor_kernel, me), out_shape=(jax.Shape...  2.11 us

commit v1 on v0

--- a/solution.py
+++ b/solution.py
@@ -21,6 +21,7 @@
 GROUPS = 16
 TYPE, MAT, RATIO, FEE, MORT, ACC, SIG, KEY = 8, 9, 10, 11, 12, 13, 14, 15
 SLAB = 24
+MESSAGES = 50
 LOG2E = 1.0 / math.log(2.0)
 UNIT = LOG2E / SMOOTH
 
@@ -78,7 +79,11 @@
     scratch[ACC : ACC + 1, 0:16] = acc_ref[...]
     scratch[SIG : SIG + 1, 0:8] = sigma_row
     scratch[KEY : KEY + 1, 0:16] = key
-    table_ref[...] = pltpu.roll(scratch[...], 16 * lax.rem(me, 8), 1)
+    for r in range(2):
+        line = scratch[8 * r : 8 * r + 1, :]
+        for k in range(1, 8):
+            line = line + pltpu.roll(scratch[8 * r + k : 8 * r + k + 1, :], 16 * k, 1)
+        table_ref[r : r + 1, :] = line
 
     rows = jnp.concatenate(
         [shocks_ref[m, :, 128 * j : 128 * j + 128] for m in range(2) for j in range(16)],
@@ -111,15 +116,15 @@
         months.append(regs)
     for g in range(16):
         both = jnp.concatenate([months[0][g], months[1][g]], axis=0)
-        out_ref[:, 128 * g : 128 * g + 128] = both.astype(BF16)
+        out_ref[g // 4, :, 128 * (g % 4) : 128 * (g % 4) + 128] = both.astype(BF16)
 
 
 def own_factor(shocks, sigma, index, alloc, *rest, me=None):
     return pl.pallas_call(
         functools.partial(factor_kernel, me),
         out_shape=(
-            jax.ShapeDtypeStruct((16, 2048), BF16),
-            jax.ShapeDtypeStruct((16, 128), F32),
+            jax.ShapeDtypeStruct((4, 16, 512), BF16),
+            jax.ShapeDtypeStruct((2, 128), F32),
         ),
         scratch_shapes=[pltpu.VMEM((16, 128), F32)],
         name="own_factor",
@@ -128,36 +133,107 @@
 
 def gather_kernel(block_ref, table_ref, blocks_ref, tables_ref, send, recv, own):
     me = lax.axis_index("outer")
+    row, col = me // 4, me % 4
+
+    def at(dy, dx):
+        return ((row + dy) % 4) * 4 + (col + dx) % 4
+
+    peers = [at(0, 1), at(0, 3), at(1, 0), at(3, 0), at(0, 2), at(2, 0)]
     barrier = pltpu.get_barrier_semaphore()
-    for d in range(1, NOUT):
-        pl.semaphore_signal(
-            barrier, inc=1, device_id={"outer": lax.rem(me + d, NOUT)}, device_id_type=MESH
+    for peer in peers:
+        pl.semaphore_signal(barrier, inc=1, device_id={"outer": peer}, device_id_type=MESH)
+    pl.semaphore_wait(barrier, len(peers))
+
+    started = []
+
+    def post(number, peer, src, dst):
+        copy = pltpu.make_async_remote_copy(
+            src_ref=src,
+            dst_ref=dst,
+            send_sem=send.at[number],
+            recv_sem=recv.at[number],
+            device_id={"outer": peer},
+            device_id_type=MESH,
         )
-    pl.semaphore_wait(barrier, NOUT - 1)
-    copies = []
-    for d in range(1, NOUT):
-        peer = lax.rem(me + d, NOUT)
-        for n, (src, dst) in enumerate(((table_ref, tables_ref), (block_ref, blocks_ref))):
-            copy = pltpu.make_async_remote_copy(
-                src_ref=src,
-                dst_ref=dst.at[me],
-                send_sem=send.at[n, d],
-                recv_sem=recv.at[n, d],
-                device_id={"outer": peer},
-                device_id_type=MESH,
-            )
-            copy.start()
-            copies.append(copy)
-    mine = [
+        copy.start()
+        started.append(copy)
+        return copy
+
+    numbers = iter(range(MESSAGES))
+
+    def piece(origin, first, count):
+        return blocks_ref.at[origin, pl.ds(first, count)]
+
+    def send_piece(peer, origin, first, count, mine=False):
+        dst = piece(origin, first, count)
+        src = block_ref.at[pl.ds(first, count)] if mine else dst
+        return post(next(numbers), peer, src, dst)
+
+    local = [
         pltpu.make_async_copy(table_ref, tables_ref.at[me], own.at[0]),
         pltpu.make_async_copy(block_ref, blocks_ref.at[me], own.at[1]),
     ]
-    for copy in mine:
+    for copy in local:
         copy.start()
-    for copy in mine:
-        copy.wait()
-    for copy in copies:
-        copy.wait()
+
+    across = [post(next(numbers), at(0, d), table_ref, tables_ref.at[me]) for d in (1, 3, 2)]
+
+    def shift(color, first_step, second_step):
+        return at(second_step, first_step) if color == 0 else at(first_step, second_step)
+
+    near = []
+    for color in range(2):
+        q = 2 * color
+        near.append([send_piece(shift(color, d, 0), me, q, 2, True) for d in (1, 3)])
+    home = []
+    for color in range(2):
+        q = 2 * color
+        home.append([send_piece(shift(color, 0, d), me, q, 2, True) for d in (1, 3)])
+
+    second = []
+    far = []
+    for side in range(2):
+        for color in range(2):
+            q = 2 * color
+            behind, onward = (3, 1) if side == 0 else (1, 3)
+            near[color][side].wait_recv()
+            origin = shift(color, behind, 0)
+            far.append((color, side, send_piece(shift(color, onward, 0), origin, q + side, 1)))
+            for way, d in enumerate((1, 3)):
+                copy = send_piece(shift(color, 0, d), origin, q, 2)
+                second.append((color, behind, q, 2, way, copy))
+
+    last = []
+
+    def hand_on(color, first, q, count, way, copy):
+        copy.wait_recv()
+        behind, onward = (3, 1) if way == 0 else (1, 3)
+        quarter = 2 * color + way
+        if not q <= quarter < q + count:
+            return
+        origin = shift(color, first, behind)
+        last.append(send_piece(shift(color, 0, onward), origin, quarter, 1))
+
+    for way in range(2):
+        for color in range(2):
+            hand_on(color, 0, 2 * color, 2, way, home[color][way])
+    for copy in across:
+        copy.wait_recv()
+    local[0].wait()
+    line = tables_ref.at[pl.ds(row * 4, 4)]
+    down = [post(next(numbers), at(d, 0), line, line) for d in (1, 3, 2)]
+    for color, side, copy in far:
+        copy.wait_recv()
+        for way, d in enumerate((1, 3)):
+            fresh = send_piece(shift(color, 0, d), shift(color, 2, 0), 2 * color + side, 1)
+            second.append((color, 2, 2 * color + side, 1, way, fresh))
+    for entry in second:
+        hand_on(*entry)
+    for copy in down + last:
+        copy.wait_recv()
+    local[1].wait()
+    for copy in started:
+        copy.wait_send()
 
 
 def gather_outer(block, table):
@@ -166,14 +242,14 @@
     return pl.pallas_call(
         gather_kernel,
         out_shape=(
-            jax.ShapeDtypeStruct((NOUT, 16, 2048), BF16),
-            jax.ShapeDtypeStruct((NOUT, 16, 128), F32),
+            jax.ShapeDtypeStruct((NOUT, 4, 16, 512), BF16),
+            jax.ShapeDtypeStruct((NOUT, 2, 128), F32),
         ),
         in_specs=[vmem, vmem],
         out_specs=(anywhere, anywhere),
         scratch_shapes=[
-            pltpu.SemaphoreType.DMA((2, NOUT)),
-            pltpu.SemaphoreType.DMA((2, NOUT)),
+            pltpu.SemaphoreType.DMA((MESSAGES,)),
+            pltpu.SemaphoreType.DMA((MESSAGES,)),
             pltpu.SemaphoreType.DMA((2,)),
         ],
         compiler_params=pltpu.CompilerParams(collective_id=0, has_side_effects=True),
@@ -201,12 +277,23 @@
     sens,
     sums_in,
     kerns,
+    dates,
     sem,
 ):
-    params_t = jnp.concatenate(
-        [sum(tables_ref[s] for s in range(8)), sum(tables_ref[s] for s in range(8, 16))],
-        axis=1,
-    )
+    lanes = iota((8, 128), 1)
+    chosen = 16 * iota((8, 128), 0) + lanes % 16
+    halves = []
+    for h in range(2):
+        pieces = []
+        for r in range(2):
+            piece = jnp.zeros((8, 128), F32)
+            for s in range(8):
+                line = jnp.broadcast_to(tables_ref[8 * h + s, r : r + 1, :], (8, 128))
+                line = jnp.take_along_axis(line, chosen, axis=1)
+                piece = jnp.where(lanes // 16 == s, line, piece)
+            pieces.append(piece)
+        halves.append(jnp.concatenate(pieces, axis=0))
+    params_t = jnp.concatenate(halves, axis=1)
     params = params_t.T
     key_col, key_row = params[:, KEY : KEY + 1], params_t[KEY : KEY + 1]
     rank_col = jnp.sum((key_row < key_col).astype(F32), axis=1, keepdims=True)
@@ -229,8 +316,9 @@
     mine = (begin <= item) & (item < begin + count)
     tile_id = iota((TILES, 384), 0).astype(F32)
     plan_v[0:1, :] = jnp.sum(jnp.where(mine, tile_id, 0.0), axis=0, keepdims=True).astype(jnp.int32)
-    place_g = jnp.where(mine, low + 2.0 * (item - begin), 0.0)
-    plan_v[1:2, :] = jnp.sum(place_g, axis=0, keepdims=True).astype(jnp.int32)
+    place_g = jnp.where(mine, low + 2.0 * (item - begin) - 16.0, 0.0)
+    place_g = 16.0 + jnp.sum(place_g, axis=0, keepdims=True)
+    plan_v[1:2, :] = place_g.astype(jnp.int32)
     items = jnp.sum(mine.astype(F32), axis=(0, 1), keepdims=True)
     plan_v[2:8, :] = jnp.broadcast_to(items, (6, 384)).astype(jnp.int32)
     copy = pltpu.make_async_copy(plan_v, plan, sem)
@@ -249,6 +337,16 @@
         level[m] = jnp.exp(total)
         rate = jnp.sum(rate_col[:, m : m + 1] * spread_o, axis=0, keepdims=True)
         rates.append(jnp.broadcast_to(rate, (8, 128)))
+
+    step_in = iota((8, 128), 0) % 4
+    for g in range(GROUPS + 2):
+        hz = (step_in + (4 * g + 1)).astype(F32)
+        for m in range(2):
+            power = (LOG2E * rates[m]) * hz
+            discount = lax.exp2(-power)
+            dates[g, 3 * m] = discount
+            dates[g, 3 * m + 1] = hz * discount
+            dates[g, 3 * m + 2] = lax.exp2(power) * UNIT
 
     fund = iota((128, 128), 0).astype(F32)
     step_in = iota((8, 128), 0) % 4
@@ -279,11 +377,11 @@
         log_keep = jnp.log(1.0 - row(MORT))
         rows_t[j, 0:1] = jnp.where(death, 1.0, mat)
         rows_t[j, 1:2] = mat
-        rows_t[j, 2:3] = jnp.where(death, row(MORT), 1.0)
-        rows_t[j, 3:4] = jnp.where(death, log_keep, 0.0) * LOG2E
-        rows_t[j, 4:5] = jnp.where(death, -log_keep, log_keep * mat) * LOG2E
-        rows_t[j, 5:6] = row(FEE) * LOG2E
-        rows_t[j, 6:7] = row(RATIO) * UNIT
+        rows_t[j, 2:3] = jnp.where(death, log_keep, 0.0) * LOG2E
+        shift = jnp.where(death, jnp.log(row(MORT)) - log_keep, log_keep * mat)
+        rows_t[j, 3:4] = shift * LOG2E
+        rows_t[j, 4:5] = row(FEE) * -LOG2E
+        rows_t[j, 5:6] = row(RATIO) * UNIT
         acc_t[pl.ds(j, 1), :] = row(ACC)
         return carry
 
@@ -291,71 +389,68 @@
 
     for g in range(GROUPS):
         cols = slice(128 * g, 128 * g + 128)
-        part = blocks_ref[:, :, cols].astype(F32).reshape(16, 2, 8, 128)
+        part = blocks_ref[:, g // 4, :, 128 * (g % 4) : 128 * (g % 4) + 128]
+        part = part.astype(F32).reshape(16, 2, 8, 128)
         for m in range(2):
             one = part[:, m].reshape(128, 128)
             fmat[m, :, cols] = one.astype(BF16)
         fmat_t[cols, :] = part.reshape(256, 128).T.astype(BF16)
-    fmat[:, :, 2048:] = jnp.zeros((2, 128, 128), BF16)
+    fmat[:, :, 2048:] = jnp.zeros((2, 128, 256), BF16)
     fmat_t[2048:, :] = jnp.zeros((256, 256), BF16)
     copy.wait()
 
-    def raw(j, g):
-        here = pl.ds(pl.multiple_of(g * 128, 128), 128)
-        return dot(fmat_t[here, :], weight_t[j])
-
-    rates2 = [rate * LOG2E for rate in rates]
-
-    def group(j, g, slot):
+    def raw(i, half):
+        here = pl.ds(pl.multiple_of(plan[1, i] * 128, 128), 256)
+        sums_in[half] = dot(fmat_t[here, :], weight_t[plan[0, i]])
+
+    def group(j, g, half, slot):
         def wide(k):
             return jnp.broadcast_to(rows_t[j, k : k + 1], (8, 128))
 
         hz = (step_in + (4 * g + 1)).astype(F32)
-        fee = wide(5)
-        decay = jnp.where(
-            (hz >= wide(0)) & (hz <= wide(1)),
-            wide(2) * lax.exp2(wide(3) * hz + wide(4)),
-            0.0,
-        )
-        fee_decay = lax.exp2(-fee * hz) * decay
-        strike = wide(6)
+        decay = lax.exp2(wide(2) * hz + wide(3))
+        decay = jnp.where((hz >= wide(0)) & (hz <= wide(1)), decay, 0.0)
+        fee_power = lax.exp2(wide(4) * hz)
+        fee_decay = fee_power * decay
+        strike = wide(5)
+        part = slice(128 * slot, 128 * slot + 128)
         for m in range(2):
-            growth = lax.exp2((rates2[m] - fee) * hz) * UNIT
-            weight = decay * lax.exp2(-rates2[m] * hz)
-            y = sums_in[slot, :, 128 * m : 128 * m + 128].reshape(16, 8, 128) * growth
-            x = strike - y
-            up = lax.exp2(x)
+            growth = fee_power * dates[g, 3 * m + 2]
+            y = sums_in[half, part, 128 * m : 128 * m + 128].reshape(16, 8, 128) * growth
+            up = lax.exp2(strike - y)
             more = 1.0 + up
             soft = jnp.where(up < 2.0**-12, up, jnp.log(more))
             slope = up / more
-            kern = (fee_decay * slope).reshape(128, 128).astype(BF16)
+            kerns[half, m, part, :] = (fee_decay * slope).reshape(128, 128).astype(BF16)
             soft_sum = jnp.sum(soft, axis=0)
             rho_sum = soft_sum + jnp.sum(slope * y, axis=0) * (1.0 / LOG2E)
-            sums_t[j, 2 * m] += weight * soft_sum
-            sums_t[j, 2 * m + 1] += (hz * weight) * rho_sum
-            kerns[m, 128 * slot : 128 * slot + 128, :] = kern
-
-    def flush(j, g):
-        here = pl.ds(pl.multiple_of(g * 128, 128), 256)
+            sums_t[j, 2 * m] += (decay * dates[g, 3 * m]) * soft_sum
+            sums_t[j, 2 * m + 1] += (decay * dates[g, 3 * m + 1]) * rho_sum
+
+    def flush(i, half):
+        j = plan[0, i]
+        here = pl.ds(pl.multiple_of(plan[1, i] * 128, 128), 256)
         for m in range(2):
-            sens[j, m] += dot(fmat[m, :, here], kerns[m])
-
-    total = plan[2, 0]
-    kerns[...] = jnp.zeros((2, 256, 128), BF16)
-    sums_in[0] = raw(plan[0, 0], plan[1, 0])
-
-    def work(i, carry):
+            sens[j, m] += dot(fmat[m, :, here], kerns[half, m])
+
+    def item_work(i, half):
         j, g = plan[0, i], plan[1, i]
-        last = jnp.maximum(i - 1, 0)
-        flush(plan[0, last], plan[1, last])
-        sums_in[1] = raw(j, g + 1)
-        group(j, g, 0)
-        sums_in[0] = raw(plan[0, i + 1], plan[1, i + 1])
-        group(j, g + 1, 1)
+        flush(jnp.maximum(i - 1, 0), 1 - half)
+        raw(i + 1, 1 - half)
+        group(j, g, half, 0)
+        group(j, g + 1, half, 1)
+
+    kerns[1] = jnp.zeros((2, 256, 128), BF16)
+    raw(0, 0)
+
+    def work(n, carry):
+        item_work(2 * n, 0)
+        item_work(2 * n + 1, 1)
         return carry
 
-    lax.fori_loop(0, total, work, 0)
-    flush(plan[0, total - 1], plan[1, total - 1])
+    pairs = (plan[2, 0] + 1) // 2
+    lax.fori_loop(0, pairs, work, 0)
+    flush(2 * pairs - 1, 1)
 
     def close(q, deltas):
         fresh = list(deltas)
@@ -398,7 +493,7 @@
         value_kernel,
         out_shape=jax.ShapeDtypeStruct((NIN, SLAB, 128), F32),
         scratch_shapes=[
-            pltpu.VMEM((2, 128, 2176), BF16),
+            pltpu.VMEM((2, 128, 2304), BF16),
             pltpu.VMEM((2304, 256), BF16),
             pltpu.VMEM((2, 128, 128), F32),
             pltpu.VMEM((TILES, 256, 256), BF16),
@@ -410,15 +505,16 @@
             pltpu.SMEM((8, 384), jnp.int32),
             pltpu.VMEM((TILES, 4, 8, 128), F32),
             pltpu.VMEM((TILES, 2, 128, 128), F32),
-            pltpu.VMEM((2, 128, 256), F32),
-            pltpu.VMEM((2, 256, 128), BF16),
+            pltpu.VMEM((2, 256, 256), F32),
+            pltpu.VMEM((2, 2, 256, 128), BF16),
+            pltpu.VMEM((GROUPS + 2, 6, 8, 128), F32),
             pltpu.SemaphoreType.DMA(()),
         ],
         name="revalue",
     )(blocks, tables, world, rate.T)
 
 
-def scatter_kernel(slabs_ref, out_ref, inbox, send, recv):
+def scatter_kernel(slabs_ref, res_ref, rho_ref, del_ref, inbox, send, recv):
     me = lax.axis_index("inner")
     barrier = pltpu.get_barrier_semaphore()
     for d in range(1, NIN):
@@ -443,16 +539,27 @@
     for d in range(1, NIN):
         copies[d - 1].wait()
         total = total + inbox[d]
-    out_ref[...] = total
+    for o in range(2):
+        for m in range(2):
+            r = o * 10 + m * 5
+            for k in range(2):
+                lanes = slice(128 * k, 128 * k + 128)
+                res_ref[o, m : m + 1, lanes] = total[r + k : r + k + 1]
+                rho_ref[o, m : m + 1, lanes] = total[r + 2 + k : r + 3 + k]
+            del_ref[o, m : m + 1, :] = total[r + 4 : r + 5]
 
 
 def scatter_inner(slabs):
     vmem = pl.BlockSpec(memory_space=pltpu.VMEM)
     return pl.pallas_call(
         scatter_kernel,
-        out_shape=jax.ShapeDtypeStruct((SLAB, 128), F32),
+        out_shape=(
+            jax.ShapeDtypeStruct((2, 2, 256), F32),
+            jax.ShapeDtypeStruct((2, 2, 256), F32),
+            jax.ShapeDtypeStruct((2, 2, 128), F32),
+        ),
         in_specs=[vmem],
-        out_specs=vmem,
+        out_specs=(vmem, vmem, vmem),
         scratch_shapes=[
             pltpu.VMEM((NIN, SLAB, 128), F32),
             pltpu.SemaphoreType.DMA((NIN,)),
@@ -491,8 +598,7 @@
     )
     blocks, tables = gather_outer(block, table)
     slabs = revalue(blocks, tables, world_shocks, short_rate)
-    total = scatter_inner(slabs)[:20].reshape(2, 2, 5 * 128)
-    return total[..., :256], total[..., 256:512], total[..., 512:]
+    return scatter_inner(slabs)
 
 
 def solution(mesh):

time: 75.1 us -> 63.4 us (0.84); the launches traced: 76.4 us -> 63.3 us
  Pallas kernels: 73.8 us -> 60 us
    pallas_call x1, Pallas kernels: 38.5 us -> 28 us  [revalue(): pl.pallas_call(value_kernel, out_shape=jax.ShapeDtypeStruct((NIN, SLAB, 1...]
    pallas_call x2, Pallas kernels: 33.2 us -> 30 us  [the longest x1 17.7 us: gather_outer(): pl.pallas_call(gather_kernel, out_shape=(jax.ShapeDtypeStruct((NOUT, 4, 1...]
    unnamed x0 -> x9, local copies, waits for them, and re-layouts: none -> 2.61 us
    slice x2 -> x0, local copies, waits for them, and re-layouts: 1.18 us -> none  [shards(): return (total[..., :256], total[..., 256:512], total[..., 512:])]
where the time goes in v1:
time: 63.4 us; the launch traced here: 63.3 us
  Pallas kernels  60 us (95%)
  local copies, waits for them, and re-layouts  2.61 us (4%)
  between operations  0.67 us (1%)
    pallas_call x1, Pallas kernels, revalue(): pl.pallas_call(value_kernel, out_shape=jax.ShapeDtypeStruct((NIN, SLAB, 1...  28 us
    pallas_call x1, Pallas kernels, gather_outer(): pl.pallas_call(gather_kernel, out_shape=(jax.ShapeDtypeStruct((NOUT, 4, 1...  17.7 us
    pallas_call x1, Pallas kernels, scatter_inner(): pl.pallas_call(scatter_kernel, out_shape=(jax.ShapeDtypeStruct((2, 2, 256...  12.3 us
    unnamed x9, local copies, waits for them, and re-layouts  2.61 us
    pallas_call x1, Pallas kernels, own_factor(): pl.pallas_call(functools.partial(factor_kernel, me), out_shape=(jax.Shape...  2.11 us

profile of v1, /device:TPU:1, one launch (start us, length us, event | category | flops | bytes accessed | tf_op | source)
XLA Modules:
  0.0 63.3 jit_solution(16528075422388148480)
XLA Ops:
  0.6 2.1 %own_factor.1 = (bf16[4,16,512]{2,1,0:T(8,128)(2,1)}, f32[2,128]{1,0:T(2,128)}) custom-call(f32[2,8,2048]{2,1,0:T(8,128)} %shocks_ref.1, f32[1,8]{1,0:T(1,128)} %bitcast.13, s32[4,16]{1,0:T(4,128)} %bitcast.10, f32[4,16]{1,0:T(4,128)} %bitcast.11, s32[1,16]{1,0:T(1,128)} %bitcast.14, s32[1,16]{1,0:T(1,128)} %bitcast.15, f32[1,16]{1,0:T(1,128)} %bitcast.16, ...), custom_call_target="tpu_custom_call" | custom-call | tf_op jit(solution)/shard_map/own_factor/pallas_call | solution.py:123
  2.7 17.7 %gather_outer.1 = (bf16[16,4,16,512]{3,2,1,0:T(8,128)(2,1)}, f32[16,2,128]{2,1,0:T(2,128)}) custom-call(bf16[4,16,512]{2,1,0:T(8,128)(2,1)} %get-tuple-element.7.block_ref, f32[2,128]{1,0:T(2,128)} %get-tuple-element.8.table_ref), custom_call_target="tpu_custom_call" | custom-call | tf_op jit(solution)/shard_map/gather_outer/pallas_call | solution.py:242
  20.4 28.0 %revalue.1.slabs_ref = f32[8,24,128]{2,1,0:T(8,128)} custom-call(bf16[16,4,16,512]{3,2,1,0:T(8,128)(2,1)} %get-tuple-element.9.blocks_ref, f32[16,2,128]{2,1,0:T(2,128)} %get-tuple-element.10.tables_ref, f32[16,2,128]{2,1,0:T(2,128)} %world_ref.1, f32[2,16]{1,0:T(2,128)} %bitcast.12), custom_call_target="tpu_custom_call" | custom-call | tf_op jit(solution)/shard_map/revalue/pallas_call | solution.py:492
  48.4 12.3 %scatter_inner.1 = (f32[2,2,256]{2,1,0:T(2,128)}, f32[2,2,256]{2,1,0:T(2,128)}, f32[2,2,128]{2,1,0:T(2,128)}) custom-call(f32[8,24,128]{2,1,0:T(8,128)} %revalue.1.slabs_ref), custom_call_target="tpu_custom_call" | custom-call | tf_op jit(solution)/shard_map/scatter_inner/pallas_call | solution.py:554
  60.7 0.0 copy-start.1
  60.7 0.7 %copy-done.1 = f32[2,2,256]{2,1,0:T(2,128)S(1)} copy-done((f32[2,2,256]{2,1,0:T(2,128)S(1)}, f32[2,2,256]{2,1,0:T(2,128)}, u32[]{:S(2)}) %copy-start.1) | copy-done | bytes 4120
  61.4 0.0 copy-start
  61.4 0.6 copy.18
  62.0 0.1 copy-done
  62.0 0.0 copy-start.2
  62.1 0.6 copy.19
  62.6 0.1 copy-done.2
  62.7 0.6 copy.20
Async XLA Ops:
  60.7 0.7 %copy-start.1 = (f32[2,2,256]{2,1,0:T(2,128)S(1)}, f32[2,2,256]{2,1,0:T(2,128)}, u32[]{:S(2)}) copy-start(f32[2,2,256]{2,1,0:T(2,128)} %get-tuple-element.14) | copy-start | bytes 12292
  61.4 0.7 %copy-start = (f32[2,2,256]{2,1,0:T(2,128)S(1)}, f32[2,2,256]{2,1,0:T(2,128)}, u32[]{:S(2)}) copy-start(f32[2,2,256]{2,1,0:T(2,128)} %get-tuple-element.15) | copy-start | bytes 12292
  62.0 0.7 %copy-start.2 = (f32[2,2,128]{2,1,0:T(2,128)S(1)}, f32[2,2,128]{2,1,0:T(2,128)}, u32[]{:S(2)}) copy-start(f32[2,2,128]{2,1,0:T(2,128)} %get-tuple-element.16) | copy-start | bytes 6148

commit v2 on v1

--- a/solution.py
+++ b/solution.py
@@ -123,163 +123,37 @@
     return pl.pallas_call(
         functools.partial(factor_kernel, me),
         out_shape=(
-            jax.ShapeDtypeStruct((4, 16, 512), BF16),
-            jax.ShapeDtypeStruct((2, 128), F32),
+            pltpu.VMEM((4, 16, 512), BF16),
+            pltpu.VMEM((2, 128), F32),
         ),
         scratch_shapes=[pltpu.VMEM((16, 128), F32)],
+        compiler_params=pltpu.CompilerParams(vmem_limit_bytes=8 << 20),
         name="own_factor",
     )(shocks, sigma[None], index.T, alloc.T, *(value[None] for value in rest))
 
 
-def gather_kernel(block_ref, table_ref, blocks_ref, tables_ref, send, recv, own):
-    me = lax.axis_index("outer")
-    row, col = me // 4, me % 4
-
-    def at(dy, dx):
-        return ((row + dy) % 4) * 4 + (col + dx) % 4
-
-    peers = [at(0, 1), at(0, 3), at(1, 0), at(3, 0), at(0, 2), at(2, 0)]
-    barrier = pltpu.get_barrier_semaphore()
-    for peer in peers:
-        pl.semaphore_signal(barrier, inc=1, device_id={"outer": peer}, device_id_type=MESH)
-    pl.semaphore_wait(barrier, len(peers))
-
-    started = []
-
-    def post(number, peer, src, dst):
-        copy = pltpu.make_async_remote_copy(
-            src_ref=src,
-            dst_ref=dst,
-            send_sem=send.at[number],
-            recv_sem=recv.at[number],
-            device_id={"outer": peer},
-            device_id_type=MESH,
-        )
-        copy.start()
-        started.append(copy)
-        return copy
-
-    numbers = iter(range(MESSAGES))
-
-    def piece(origin, first, count):
-        return blocks_ref.at[origin, pl.ds(first, count)]
-
-    def send_piece(peer, origin, first, count, mine=False):
-        dst = piece(origin, first, count)
-        src = block_ref.at[pl.ds(first, count)] if mine else dst
-        return post(next(numbers), peer, src, dst)
-
-    local = [
-        pltpu.make_async_copy(table_ref, tables_ref.at[me], own.at[0]),
-        pltpu.make_async_copy(block_ref, blocks_ref.at[me], own.at[1]),
-    ]
-    for copy in local:
-        copy.start()
-
-    across = [post(next(numbers), at(0, d), table_ref, tables_ref.at[me]) for d in (1, 3, 2)]
-
-    def shift(color, first_step, second_step):
-        return at(second_step, first_step) if color == 0 else at(first_step, second_step)
-
-    near = []
-    for color in range(2):
-        q = 2 * color
-        near.append([send_piece(shift(color, d, 0), me, q, 2, True) for d in (1, 3)])
-    home = []
-    for color in range(2):
-        q = 2 * color
-        home.append([send_piece(shift(color, 0, d), me, q, 2, True) for d in (1, 3)])
-
-    second = []
-    far = []
-    for side in range(2):
-        for color in range(2):
-            q = 2 * color
-            behind, onward = (3, 1) if side == 0 else (1, 3)
-            near[color][side].wait_recv()
-            origin = shift(color, behind, 0)
-            far.append((color, side, send_piece(shift(color, onward, 0), origin, q + side, 1)))
-            for way, d in enumerate((1, 3)):
-                copy = send_piece(shift(color, 0, d), origin, q, 2)
-                second.append((color, behind, q, 2, way, copy))
-
-    last = []
-
-    def hand_on(color, first, q, count, way, copy):
-        copy.wait_recv()
-        behind, onward = (3, 1) if way == 0 else (1, 3)
-        quarter = 2 * color + way
-        if not q <= quarter < q + count:
-            return
-        origin = shift(color, first, behind)
-        last.append(send_piece(shift(color, 0, onward), origin, quarter, 1))
-
-    for way in range(2):
-        for color in range(2):
-            hand_on(color, 0, 2 * color, 2, way, home[color][way])
-    for copy in across:
-        copy.wait_recv()
-    local[0].wait()
-    line = tables_ref.at[pl.ds(row * 4, 4)]
-    down = [post(next(numbers), at(d, 0), line, line) for d in (1, 3, 2)]
-    for color, side, copy in far:
-        copy.wait_recv()
-        for way, d in enumerate((1, 3)):
-            fresh = send_piece(shift(color, 0, d), shift(color, 2, 0), 2 * color + side, 1)
-            second.append((color, 2, 2 * color + side, 1, way, fresh))
-    for entry in second:
-        hand_on(*entry)
-    for copy in down + last:
-        copy.wait_recv()
-    local[1].wait()
-    for copy in started:
-        copy.wait_send()
-
-
-def gather_outer(block, table):
-    vmem = pl.BlockSpec(memory_space=pltpu.VMEM)
-    anywhere = pl.BlockSpec(memory_space=pl.ANY)
-    return pl.pallas_call(
-        gather_kernel,
-        out_shape=(
-            jax.ShapeDtypeStruct((NOUT, 4, 16, 512), BF16),
-            jax.ShapeDtypeStruct((NOUT, 2, 128), F32),
-        ),
-        in_specs=[vmem, vmem],
-        out_specs=(anywhere, anywhere),
-        scratch_shapes=[
-            pltpu.SemaphoreType.DMA((MESSAGES,)),
-            pltpu.SemaphoreType.DMA((MESSAGES,)),
-            pltpu.SemaphoreType.DMA((2,)),
-        ],
-        compiler_params=pltpu.CompilerParams(collective_id=0, has_side_effects=True),
-        name="gather_outer",
-    )(block, table)
-
-
-def value_kernel(
-    blocks_ref,
-    tables_ref,
-    world_ref,
-    rate_ref,
-    out_ref,
-    fmat,
-    fmat_t,
-    level,
-    weight_t,
-    dwt,
-    rows_t,
-    acc_t,
-    table,
-    plan_v,
-    plan,
-    sums_t,
-    sens,
-    sums_in,
-    kerns,
-    dates,
-    sem,
-):
+def spread():
+    return (iota((16, 128), 1) % 16 == iota((16, 128), 0)).astype(F32)
+
+
+def date_tables(rate_ref, dates):
+    rate_col = rate_ref[...].T
+    rates = []
+    for m in range(2):
+        rate = jnp.sum(rate_col[:, m : m + 1] * spread(), axis=0, keepdims=True)
+        rates.append(jnp.broadcast_to(rate, (8, 128)))
+    step_in = iota((8, 128), 0) % 4
+    for g in range(GROUPS + 2):
+        hz = (step_in + (4 * g + 1)).astype(F32)
+        for m in range(2):
+            power = (LOG2E * rates[m]) * hz
+            discount = lax.exp2(-power)
+            dates[g, 3 * m] = discount
+            dates[g, 3 * m + 1] = hz * discount
+            dates[g, 3 * m + 2] = lax.exp2(power) * UNIT
+
+
+def cohort_order(tables_ref, table, plan_v, rank_ref):
     lanes = iota((8, 128), 1)
     chosen = 16 * iota((8, 128), 0) + lanes % 16
     halves = []
@@ -300,6 +174,7 @@
     rank_row = jnp.sum((key_col < key_row).astype(F32), axis=0, keepdims=True)
     place = (rank_col == iota((256, 256), 1).astype(F32)).astype(F32)
     ordered = dot01(params_t, place)
+    rank_ref[...] = jnp.broadcast_to(rank_row, (8, 256))
     table[0] = ordered[:, :128]
     table[1] = ordered[:, 128:]
 
@@ -321,35 +196,23 @@
     plan_v[1:2, :] = place_g.astype(jnp.int32)
     items = jnp.sum(mine.astype(F32), axis=(0, 1), keepdims=True)
     plan_v[2:8, :] = jnp.broadcast_to(items, (6, 384)).astype(jnp.int32)
-    copy = pltpu.make_async_copy(plan_v, plan, sem)
-    copy.start()
-
-    spread_o = (iota((16, 128), 1) % 16 == iota((16, 128), 0)).astype(F32)
+    return params
+
+
+def fund_levels(params, world_ref, level):
+    spread_o = spread()
     sigma = params[:, SIG : SIG + 1].reshape(16, 2, 8, 1)[:, 0].reshape(128, 1)
     total = jnp.zeros((128, 128), F32)
-    rates = []
-    rate_col = rate_ref[...].T
     for m in range(2):
         shock = dot01(world_ref[:, m, :], spread_o, ((0,), (0,)))
         total = total + (
             (DRIFT - 0.5 * sigma * sigma) / 12.0 + sigma * shock / math.sqrt(12.0)
         )
         level[m] = jnp.exp(total)
-        rate = jnp.sum(rate_col[:, m : m + 1] * spread_o, axis=0, keepdims=True)
-        rates.append(jnp.broadcast_to(rate, (8, 128)))
-
-    step_in = iota((8, 128), 0) % 4
-    for g in range(GROUPS + 2):
-        hz = (step_in + (4 * g + 1)).astype(F32)
-        for m in range(2):
-            power = (LOG2E * rates[m]) * hz
-            discount = lax.exp2(-power)
-            dates[g, 3 * m] = discount
-            dates[g, 3 * m + 1] = hz * discount
-            dates[g, 3 * m + 2] = lax.exp2(power) * UNIT
-
+
+
+def build_tiles(first_tile, count, table, level, weight_t, dwt, rows_t, acc_t):
     fund = iota((128, 128), 0).astype(F32)
-    step_in = iota((8, 128), 0) % 4
 
     def build(j, carry):
         where = 8 * lax.rem(j, 16) + iota((16, 128), 1) // 16
@@ -369,9 +232,6 @@
             both = [one, zero] if m == 0 else [zero, one]
             both = jnp.stack(both, axis=1).reshape(256, 128)
             weight_t[j, :, 128 * m : 128 * m + 128] = both.astype(BF16)
-            sens[j, m] = jnp.zeros((128, 128), F32)
-        for n in range(4):
-            sums_t[j, n] = jnp.zeros((8, 128), F32)
         death = row(TYPE) == 0.0
         mat = row(MAT)
         log_keep = jnp.log(1.0 - row(MORT))
@@ -385,7 +245,202 @@
         acc_t[pl.ds(j, 1), :] = row(ACC)
         return carry
 
-    lax.fori_loop(0, TILES, build, 0)
+    lax.fori_loop(first_tile, first_tile + count, build, 0, unroll=2)
+
+
+def gather_kernel(
+    block_ref,
+    table_ref,
+    world_ref,
+    rate_ref,
+    blocks_ref,
+    weight_t,
+    dwt,
+    rows_t,
+    acc_t,
+    dates,
+    plan_v,
+    rank_ref,
+    tables_ref,
+    table,
+    level,
+    send,
+    recv,
+    own,
+):
+    me = lax.axis_index("outer")
+    row, col = me // 4, me % 4
+
+    def at(dy, dx):
+        return ((row + dy) % 4) * 4 + (col + dx) % 4
+
+    peers = [at(0, 1), at(0, 3), at(1, 0), at(3, 0), at(0, 2), at(2, 0)]
+    barrier = pltpu.get_barrier_semaphore()
+    for peer in peers:
+        pl.semaphore_signal(barrier, inc=1, device_id={"outer": peer}, device_id_type=MESH)
+    pl.semaphore_wait(barrier, len(peers))
+
+    started = []
+
+    def post(number, peer, src, dst):
+        copy = pltpu.make_async_remote_copy(
+            src_ref=src,
+            dst_ref=dst,
+            send_sem=send.at[number],
+            recv_sem=recv.at[number],
+            device_id={"outer": peer},
+            device_id_type=MESH,
+        )
+        copy.start()
+        started.append(copy)
+        return copy
+
+    numbers = iter(range(MESSAGES))
+
+    def piece(origin, first, count):
+        return blocks_ref.at[origin, pl.ds(first, count)]
+
+    def send_piece(peer, origin, first, count, mine=False):
+        dst = piece(origin, first, count)
+        src = block_ref.at[pl.ds(first, count)] if mine else dst
+        return post(next(numbers), peer, src, dst)
+
+    local = [
+        pltpu.make_async_copy(table_ref, tables_ref.at[me], own.at[0]),
+        pltpu.make_async_copy(block_ref, blocks_ref.at[me], own.at[1]),
+    ]
+    for copy in local:
+        copy.start()
+
+    across = [post(next(numbers), at(0, d), table_ref, tables_ref.at[me]) for d in (1, 3, 2)]
+
+    def shift(color, first_step, second_step):
+        return at(second_step, first_step) if color == 0 else at(first_step, second_step)
+
+    near = []
+    for color in range(2):
+        q = 2 * color
+        near.append([send_piece(shift(color, d, 0), me, q, 2, True) for d in (1, 3)])
+    home = []
+    for color in range(2):
+        q = 2 * color
+        home.append([send_piece(shift(color, 0, d), me, q, 2, True) for d in (1, 3)])
+
+    date_tables(rate_ref, dates)
+
+    second = []
+    far = []
+    for side in range(2):
+        for color in range(2):
+            q = 2 * color
+            behind, onward = (3, 1) if side == 0 else (1, 3)
+            near[color][side].wait_recv()
+            origin = shift(color, behind, 0)
+            far.append((color, side, send_piece(shift(color, onward, 0), origin, q + side, 1)))
+            for way, d in enumerate((1, 3)):
+                copy = send_piece(shift(color, 0, d), origin, q, 2)
+                second.append((color, behind, q, 2, way, copy))
+
+    last = []
+
+    def hand_on(color, first, q, count, way, copy):
+        copy.wait_recv()
+        behind, onward = (3, 1) if way == 0 else (1, 3)
+        quarter = 2 * color + way
+        if not q <= quarter < q + count:
+            return
+        origin = shift(color, first, behind)
+        last.append(send_piece(shift(color, 0, onward), origin, quarter, 1))
+
+    for way in range(2):
+        for color in range(2):
+            hand_on(color, 0, 2 * color, 2, way, home[color][way])
+    for copy in across:
+        copy.wait_recv()
+    local[0].wait()
+    line = tables_ref.at[pl.ds(row * 4, 4)]
+    down = [post(next(numbers), at(d, 0), line, line) for d in (1, 3, 2)]
+    for color, side, copy in far:
+        copy.wait_recv()
+        for way, d in enumerate((1, 3)):
+            fresh = send_piece(shift(color, 0, d), shift(color, 2, 0), 2 * color + side, 1)
+            second.append((color, 2, 2 * color + side, 1, way, fresh))
+    for copy in down:
+        copy.wait_recv()
+    params = cohort_order(tables_ref, table, plan_v, rank_ref)
+    fund_levels(params, world_ref, level)
+    for n, entry in enumerate(second):
+        hand_on(*entry)
+        if n % 2 == 0:
+            build_tiles(2 * n, 4, table, level, weight_t, dwt, rows_t, acc_t)
+    for copy in last:
+        copy.wait_recv()
+    local[1].wait()
+    for copy in started:
+        copy.wait_send()
+
+
+def in_vmem(*arrays):
+    return [pltpu.with_memory_space_constraint(array, pltpu.VMEM) for array in arrays]
+
+
+def gather_outer(block, table, world, rate):
+    vmem = pl.BlockSpec(memory_space=pltpu.VMEM)
+    out_shape = (
+        pltpu.VMEM((NOUT, 4, 16, 512), BF16),
+        pltpu.VMEM((TILES, 256, 256), BF16),
+        pltpu.VMEM((TILES, 128, 128), F32),
+        pltpu.VMEM((TILES, 8, 128), F32),
+        pltpu.VMEM((TILES, 128), F32),
+        pltpu.VMEM((GROUPS + 2, 6, 8, 128), F32),
+        pltpu.VMEM((8, 384), jnp.int32),
+        pltpu.VMEM((8, 256), F32),
+    )
+    return pl.pallas_call(
+        gather_kernel,
+        out_shape=out_shape,
+        in_specs=[vmem] * 4,
+        out_specs=(vmem,) * len(out_shape),
+        scratch_shapes=[
+            pltpu.VMEM((NOUT, 2, 128), F32),
+            pltpu.VMEM((2, 16, 128), F32),
+            pltpu.VMEM((2, 128, 128), F32),
+            pltpu.SemaphoreType.DMA((MESSAGES,)),
+            pltpu.SemaphoreType.DMA((MESSAGES,)),
+            pltpu.SemaphoreType.DMA((2,)),
+        ],
+        compiler_params=pltpu.CompilerParams(
+            collective_id=0, has_side_effects=True, vmem_limit_bytes=24 << 20
+        ),
+        name="gather_outer",
+    )(*in_vmem(block, table), world, rate.T)
+
+
+def value_kernel(
+    blocks_ref,
+    weight_t,
+    dwt,
+    rows_t,
+    acc_t,
+    dates,
+    plan_v,
+    rank_ref,
+    out_ref,
+    fmat,
+    fmat_t,
+    plan,
+    sums_t,
+    sens,
+    sums_in,
+    kerns,
+    sem,
+):
+    copy = pltpu.make_async_copy(plan_v, plan, sem)
+    copy.start()
+    step_in = iota((8, 128), 0) % 4
+    for j in range(TILES):
+        sens[j] = jnp.zeros((2, 128, 128), F32)
+        sums_t[j] = jnp.zeros((4, 8, 128), F32)
 
     for g in range(GROUPS):
         cols = slice(128 * g, 128 * g + 128)
@@ -468,6 +523,7 @@
         value = jnp.sum(sums_t[:, n], axis=1)
         res_acc.append(value * (scale if n % 2 == 0 else -scale))
 
+    rank_row = rank_ref[0:1, :]
     tile_row = jnp.floor(rank_row * 0.125)
     slot_row = rank_row - 8.0 * tile_row
     pick = (tile_row == iota((TILES, 256), 0).astype(F32)).astype(F32)
@@ -488,42 +544,40 @@
         out_ref[b, 20:SLAB, :] = jnp.zeros((SLAB - 20, 128), F32)
 
 
-def revalue(blocks, tables, world, rate):
+def revalue(*tables):
+    vmem = pl.BlockSpec(memory_space=pltpu.VMEM)
     return pl.pallas_call(
         value_kernel,
-        out_shape=jax.ShapeDtypeStruct((NIN, SLAB, 128), F32),
+        out_shape=pltpu.VMEM((NIN, SLAB, 128), F32),
+        in_specs=[vmem] * len(tables),
+        out_specs=vmem,
         scratch_shapes=[
             pltpu.VMEM((2, 128, 2304), BF16),
             pltpu.VMEM((2304, 256), BF16),
-            pltpu.VMEM((2, 128, 128), F32),
-            pltpu.VMEM((TILES, 256, 256), BF16),
-            pltpu.VMEM((TILES, 128, 128), F32),
-            pltpu.VMEM((TILES, 8, 128), F32),
-            pltpu.VMEM((TILES, 128), F32),
-            pltpu.VMEM((2, 16, 128), F32),
-            pltpu.VMEM((8, 384), jnp.int32),
             pltpu.SMEM((8, 384), jnp.int32),
             pltpu.VMEM((TILES, 4, 8, 128), F32),
             pltpu.VMEM((TILES, 2, 128, 128), F32),
             pltpu.VMEM((2, 256, 256), F32),
             pltpu.VMEM((2, 2, 256, 128), BF16),
-            pltpu.VMEM((GROUPS + 2, 6, 8, 128), F32),
             pltpu.SemaphoreType.DMA(()),
         ],
+        compiler_params=pltpu.CompilerParams(vmem_limit_bytes=32 << 20),
         name="revalue",
-    )(blocks, tables, world, rate.T)
-
-
-def scatter_kernel(slabs_ref, res_ref, rho_ref, del_ref, inbox, send, recv):
+    )(*in_vmem(*tables))
+
+
+def scatter_kernel(slabs_ref, inbox, send, recv, own):
     me = lax.axis_index("inner")
     barrier = pltpu.get_barrier_semaphore()
     for d in range(1, NIN):
         pl.semaphore_signal(
             barrier, inc=1, device_id={"inner": lax.rem(me + d, NIN)}, device_id_type=MESH
         )
+    local = pltpu.make_async_copy(slabs_ref.at[me], inbox.at[0], own)
+    local.start()
     pl.semaphore_wait(barrier, NIN - 1)
     copies = []
-    for d in range(1, NIN):
+    for d in (4, 3, 5, 2, 6, 7, 1):
         peer = lax.rem(me + d, NIN)
         copy = pltpu.make_async_remote_copy(
             src_ref=slabs_ref.at[peer],
@@ -535,10 +589,15 @@
         )
         copy.start()
         copies.append(copy)
-    total = slabs_ref[me]
+    local.wait()
+    for copy in copies:
+        copy.wait()
+
+
+def total_kernel(inbox_ref, res_ref, rho_ref, del_ref):
+    total = inbox_ref[0]
     for d in range(1, NIN):
-        copies[d - 1].wait()
-        total = total + inbox[d]
+        total = total + inbox_ref[d]
     for o in range(2):
         for m in range(2):
             r = o * 10 + m * 5
@@ -551,8 +610,23 @@
 
 def scatter_inner(slabs):
     vmem = pl.BlockSpec(memory_space=pltpu.VMEM)
+    inbox = pl.pallas_call(
+        scatter_kernel,
+        out_shape=pltpu.VMEM((NIN, SLAB, 128), F32),
+        in_specs=[vmem],
+        out_specs=vmem,
+        scratch_shapes=[
+            pltpu.SemaphoreType.DMA((NIN,)),
+            pltpu.SemaphoreType.DMA((NIN,)),
+            pltpu.SemaphoreType.DMA(()),
+        ],
+        compiler_params=pltpu.CompilerParams(
+            collective_id=1, has_side_effects=True, vmem_limit_bytes=8 << 20
+        ),
+        name="scatter_inner",
+    )(*in_vmem(slabs))
     return pl.pallas_call(
-        scatter_kernel,
+        total_kernel,
         out_shape=(
             jax.ShapeDtypeStruct((2, 2, 256), F32),
             jax.ShapeDtypeStruct((2, 2, 256), F32),
@@ -560,14 +634,9 @@
         ),
         in_specs=[vmem],
         out_specs=(vmem, vmem, vmem),
-        scratch_shapes=[
-            pltpu.VMEM((NIN, SLAB, 128), F32),
-            pltpu.SemaphoreType.DMA((NIN,)),
-            pltpu.SemaphoreType.DMA((NIN,)),
-        ],
-        compiler_params=pltpu.CompilerParams(collective_id=1, has_side_effects=True),
-        name="scatter_inner",
-    )(slabs)
+        compiler_params=pltpu.CompilerParams(vmem_limit_bytes=8 << 20),
+        name="total_inner",
+    )(*in_vmem(inbox))
 
 
 def shards(
@@ -596,8 +665,7 @@
         mortality,
         account,
     )
-    blocks, tables = gather_outer(block, table)
-    slabs = revalue(blocks, tables, world_shocks, short_rate)
+    slabs = revalue(*gather_outer(block, table, world_shocks, short_rate))
     return scatter_inner(slabs)
 
 

time: 63.4 us -> 59.1 us (0.932)
  Pallas kernels: 60 us -> 49.9 us
  local copies, waits for them, and re-layouts: 2.61 us -> 8.23 us
    pallas_call x4 -> x5, Pallas kernels: 60 us -> 49.9 us  [the longest x1 20.5 us: revalue(): pl.pallas_call(value_kernel, out_shape=pltpu.VMEM((NIN, SLAB, 128), F32),...]
    unnamed x9 -> x24, local copies, waits for them, and re-layouts: 2.61 us -> 8.23 us
where the time goes in v2:
time: 59.1 us; the launch traced here: 58.8 us
  Pallas kernels  49.9 us (84%)
  local copies, waits for them, and re-layouts  8.23 us (14%)
  between operations  0.69 us (1%)
    pallas_call x1, Pallas kernels, revalue(): pl.pallas_call(value_kernel, out_shape=pltpu.VMEM((NIN, SLAB, 128), F32),...  20.5 us
    pallas_call x1, Pallas kernels, gather_outer(): pl.pallas_call(gather_kernel, out_shape=out_shape, in_specs=[vmem] * 4, o...  17.5 us
    pallas_call x1, Pallas kernels, scatter_inner(): pl.pallas_call(scatter_kernel, out_shape=pltpu.VMEM((NIN, SLAB, 128), F32...  10.7 us
    unnamed x24, local copies, waits for them, and re-layouts  8.23 us

profile of v2, /device:TPU:1, one launch (start us, length us, event | category | flops | bytes accessed | tf_op | source)
XLA Modules:
  0.0 58.8 jit_solution(16724196147618980326)
XLA Ops:
  0.6 0.0 copy-start
  0.6 0.9 %copy-done = f32[2,8,2048]{2,1,0:T(8,128)S(1)} copy-done((f32[2,8,2048]{2,1,0:T(8,128)S(1)}, f32[2,8,2048]{2,1,0:T(8,128)}, u32[]{:S(2)}) %copy-start) | copy-done | bytes 131096
  1.5 0.0 copy-start.2
  1.5 0.7 %copy-done.2 = s32[16,4]{0,1:T(4,128)S(1)} copy-done((s32[16,4]{0,1:T(4,128)S(1)}, s32[16,4]{0,1:T(4,128)}, u32[]{:S(2)}) %copy-start.2) | copy-done | bytes 280
  2.2 0.0 copy-start.3
  2.2 0.7 %copy-done.3 = f32[16,4]{0,1:T(4,128)S(1)} copy-done((f32[16,4]{0,1:T(4,128)S(1)}, f32[16,4]{0,1:T(4,128)}, u32[]{:S(2)}) %copy-start.3) | copy-done | bytes 280
  2.9 0.0 copy-start.5
  2.9 0.7 %copy-done.5 = f32[8]{0:T(128)S(1)} copy-done((f32[8]{0:T(128)S(1)}, f32[8]{0:T(128)}, u32[]{:S(2)}) %copy-start.5) | copy-done | bytes 56
  3.6 0.0 copy-start.6
  3.6 0.7 %copy-done.6 = s32[16]{0:T(128)S(1)} copy-done((s32[16]{0:T(128)S(1)}, s32[16]{0:T(128)}, u32[]{:S(2)}) %copy-start.6) | copy-done | bytes 88
  4.2 0.0 copy-start.7
  4.2 0.7 %copy-done.7 = s32[16]{0:T(128)S(1)} copy-done((s32[16]{0:T(128)S(1)}, s32[16]{0:T(128)}, u32[]{:S(2)}) %copy-start.7) | copy-done | bytes 88
  4.9 0.0 copy-start.8
  4.9 0.7 %copy-done.8 = f32[16]{0:T(128)S(1)} copy-done((f32[16]{0:T(128)S(1)}, f32[16]{0:T(128)}, u32[]{:S(2)}) %copy-start.8) | copy-done | bytes 88
  5.5 0.0 copy-start.9
  5.5 0.7 %copy-done.9 = f32[16]{0:T(128)S(1)} copy-done((f32[16]{0:T(128)S(1)}, f32[16]{0:T(128)}, u32[]{:S(2)}) %copy-start.9) | copy-done | bytes 88
  6.2 0.0 copy-start.10
  6.2 0.7 %copy-done.10 = f32[16]{0:T(128)S(1)} copy-done((f32[16]{0:T(128)S(1)}, f32[16]{0:T(128)}, u32[]{:S(2)}) %copy-start.10) | copy-done | bytes 88
  6.8 0.0 copy-start.11
  6.8 0.7 %copy-done.11 = f32[16]{0:T(128)S(1)} copy-done((f32[16]{0:T(128)S(1)}, f32[16]{0:T(128)}, u32[]{:S(2)}) %copy-start.11) | copy-done | bytes 88
  7.5 0.5 own_factor.1
  8.0 0.0 copy-start.1
  8.0 0.7 %copy-done.1 = f32[16,2,128]{2,1,0:T(2,128)S(1)} copy-done((f32[16,2,128]{2,1,0:T(2,128)S(1)}, f32[16,2,128]{2,1,0:T(2,128)}, u32[]{:S(2)}) %copy-start.1) | copy-done | bytes 16408
  8.7 0.0 copy-start.4
  8.7 0.7 %copy-done.4 = f32[16,2]{0,1:T(2,128)S(1)} copy-done((f32[16,2]{0,1:T(2,128)S(1)}, f32[16,2]{0,1:T(2,128)}, u32[]{:S(2)}) %copy-start.4) | copy-done | bytes 152
  9.4 17.5 %gather_outer.1 = (bf16[16,4,16,512]{3,2,1,0:T(8,128)(2,1)S(1)}, bf16[32,256,256]{2,1,0:T(8,128)(2,1)S(1)}, f32[32,128,128]{2,1,0:T(8,128)S(1)}, f32[32,8,128]{2...) custom-call(bf16[4,16,512]{2,1,0:T(8,128)(2,1)S(1)} %get-tuple-eleme, ...), custom_call_target="tpu_custom_call" | custom-call | tf_op jit(solution)/shard_map/gather_outer/pallas_call | solution.py:399
  27.0 20.5 %revalue.1.slabs_ref = f32[8,24,128]{2,1,0:T(8,128)S(1)} custom-call(bf16[16,4,16,512]{3,2,1,0:T(8,128)(2,1)S(1)} %get-tuple-element.15.blocks_ref, bf16[32,256,256]{2,1,0:T(8,128)(2,1)S(1)} %get-tuple-element.16.weight_t, f32[32,128,128]{2,1,0:T(8,128)S(1)} %get-tuple-element.17.dwt, f32[32,8,128]{2,1,0:T(8,128)S(1)} %get-tuple-element.18.rows_t, ...), custom_call_target="tpu_custom_call" | custom-call | tf_op jit(solution)/shard_map/revalue/pallas_call | solution.py:549
  47.5 10.7 %scatter_inner.1.inbox_ref = f32[8,24,128]{2,1,0:T(8,128)S(1)} custom-call(f32[8,24,128]{2,1,0:T(8,128)S(1)} %revalue.1.slabs_ref), custom_call_target="tpu_custom_call" | custom-call | tf_op jit(solution)/shard_map/scatter_inner/pallas_call | solution.py:613
  58.2 0.6 %total_inner.1 = (f32[2,2,256]{2,1,0:T(2,128)}, f32[2,2,256]{2,1,0:T(2,128)}, f32[2,2,128]{2,1,0:T(2,128)}) custom-call(f32[8,24,128]{2,1,0:T(8,128)S(1)} %scatter_inner.1.inbox_ref), custom_call_target="tpu_custom_call" | custom-call | tf_op jit(solution)/shard_map/total_inner/pallas_call | solution.py:628
Async XLA Ops:
  0.6 0.9 %copy-start = (f32[2,8,2048]{2,1,0:T(8,128)S(1)}, f32[2,8,2048]{2,1,0:T(8,128)}, u32[]{:S(2)}) copy-start(f32[2,8,2048]{2,1,0:T(8,128)} %shocks_ref.1) | copy-start | bytes 393220
  1.5 0.7 %copy-start.2 = (s32[16,4]{0,1:T(4,128)S(1)}, s32[16,4]{0,1:T(4,128)}, u32[]{:S(2)}) copy-start(s32[16,4]{0,1:T(4,128)} %param.16) | copy-start | bytes 772
  2.2 0.7 %copy-start.3 = (f32[16,4]{0,1:T(4,128)S(1)}, f32[16,4]{0,1:T(4,128)}, u32[]{:S(2)}) copy-start(f32[16,4]{0,1:T(4,128)} %param.17) | copy-start | bytes 772
  2.9 0.7 %copy-start.5 = (f32[8]{0:T(128)S(1)}, f32[8]{0:T(128)}, u32[]{:S(2)}) copy-start(f32[8]{0:T(128)} %param.15) | copy-start | bytes 100
  3.6 0.7 %copy-start.6 = (s32[16]{0:T(128)S(1)}, s32[16]{0:T(128)}, u32[]{:S(2)}) copy-start(s32[16]{0:T(128)} %param.18) | copy-start | bytes 196
  4.2 0.7 %copy-start.7 = (s32[16]{0:T(128)S(1)}, s32[16]{0:T(128)}, u32[]{:S(2)}) copy-start(s32[16]{0:T(128)} %param.19) | copy-start | bytes 196
  4.9 0.7 %copy-start.8 = (f32[16]{0:T(128)S(1)}, f32[16]{0:T(128)}, u32[]{:S(2)}) copy-start(f32[16]{0:T(128)} %param.20) | copy-start | bytes 196
  5.5 0.7 %copy-start.9 = (f32[16]{0:T(128)S(1)}, f32[16]{0:T(128)}, u32[]{:S(2)}) copy-start(f32[16]{0:T(128)} %param.21) | copy-start | bytes 196
  6.2 0.7 %copy-start.10 = (f32[16]{0:T(128)S(1)}, f32[16]{0:T(128)}, u32[]{:S(2)}) copy-start(f32[16]{0:T(128)} %param.22) | copy-start | bytes 196
  6.8 0.7 %copy-start.11 = (f32[16]{0:T(128)S(1)}, f32[16]{0:T(128)}, u32[]{:S(2)}) copy-start(f32[16]{0:T(128)} %param.23) | copy-start | bytes 196
  8.0 0.7 %copy-start.1 = (f32[16,2,128]{2,1,0:T(2,128)S(1)}, f32[16,2,128]{2,1,0:T(2,128)}, u32[]{:S(2)}) copy-start(f32[16,2,128]{2,1,0:T(2,128)} %world_ref.1) | copy-start | bytes 49156
  8.7 0.7 %copy-start.4 = (f32[16,2]{0,1:T(2,128)S(1)}, f32[16,2]{0,1:T(2,128)}, u32[]{:S(2)}) copy-start(f32[16,2]{0,1:T(2,128)} %param.13) | copy-start | bytes 388

commit v3 on v2

--- a/solution.py
+++ b/solution.py
@@ -30,6 +30,14 @@
     return lax.dot_general(
         a, b, (dims, ((), ())), precision=precision, preferred_element_type=F32
     )
+
+
+def in_vmem(*arrays):
+    return [pltpu.with_memory_space_constraint(array, pltpu.VMEM) for array in arrays]
+
+
+def in_hbm(*arrays):
+    return [pltpu.with_memory_space_constraint(array, pltpu.HBM) for array in arrays]
 
 
 def dot01(a, b, dims=((1,), (0,)), parts=3):
@@ -129,7 +137,7 @@
         scratch_shapes=[pltpu.VMEM((16, 128), F32)],
         compiler_params=pltpu.CompilerParams(vmem_limit_bytes=8 << 20),
         name="own_factor",
-    )(shocks, sigma[None], index.T, alloc.T, *(value[None] for value in rest))
+    )(*in_hbm(shocks, sigma[None], index.T, alloc.T, *(value[None] for value in rest)))
 
 
 def spread():
@@ -378,10 +386,6 @@
     local[1].wait()
     for copy in started:
         copy.wait_send()
-
-
-def in_vmem(*arrays):
-    return [pltpu.with_memory_space_constraint(array, pltpu.VMEM) for array in arrays]
 
 
 def gather_outer(block, table, world, rate):
@@ -413,7 +417,7 @@
             collective_id=0, has_side_effects=True, vmem_limit_bytes=24 << 20
         ),
         name="gather_outer",
-    )(*in_vmem(block, table), world, rate.T)
+    )(*in_vmem(block, table), *in_hbm(world, rate.T))
 
 
 def value_kernel(
@@ -474,10 +478,15 @@
             y = sums_in[half, part, 128 * m : 128 * m + 128].reshape(16, 8, 128) * growth
             up = lax.exp2(strike - y)
             more = 1.0 + up
-            soft = jnp.where(up < 2.0**-12, up, jnp.log(more))
             slope = up / more
+            some = jnp.concatenate(
+                [up[0:4] + up[4:8] + up[8:12], up[12:14] + up[14:16]], axis=0
+            )
+            many = jnp.concatenate(
+                [more[0:4] * more[4:8] * more[8:12], more[12:14] * more[14:16]], axis=0
+            )
+            soft_sum = jnp.sum(jnp.where(some < 2.0**-12, some, jnp.log(many)), axis=0)
             kerns[half, m, part, :] = (fee_decay * slope).reshape(128, 128).astype(BF16)
-            soft_sum = jnp.sum(soft, axis=0)
             rho_sum = soft_sum + jnp.sum(slope * y, axis=0) * (1.0 / LOG2E)
             sums_t[j, 2 * m] += (decay * dates[g, 3 * m]) * soft_sum
             sums_t[j, 2 * m + 1] += (decay * dates[g, 3 * m + 1]) * rho_sum

time: 59.1 us -> 52.5 us (0.89)
  local copies, waits for them, and re-layouts: 8.23 us -> 0 us
  Pallas kernels: 49.9 us -> 51.1 us
    unnamed x24 -> x0, local copies, waits for them, and re-layouts: 8.23 us -> none
    pallas_call x1, Pallas kernels: 0.5 us -> 1.48 us  [own_factor(): pl.pallas_call(functools.partial(factor_kernel, me), out_shape=(pltpu.VME...]
    pallas_call x1, Pallas kernels: 17.5 us -> 18.3 us  [gather_outer(): pl.pallas_call(gather_kernel, out_shape=out_shape, in_specs=[vmem] * 4, o...]
where the time goes in v3:
time: 52.5 us; the launch traced here: 51.7 us
  Pallas kernels  51.1 us (97%)
  between operations  0.67 us (1%)
    pallas_call x1, Pallas kernels, revalue(): pl.pallas_call(value_kernel, out_shape=pltpu.VMEM((NIN, SLAB, 128), F32),...  20 us
    pallas_call x1, Pallas kernels, gather_outer(): pl.pallas_call(gather_kernel, out_shape=out_shape, in_specs=[vmem] * 4, o...  18.3 us
    pallas_call x1, Pallas kernels, scatter_inner(): pl.pallas_call(scatter_kernel, out_shape=pltpu.VMEM((NIN, SLAB, 128), F32...  10.7 us
    pallas_call x1, Pallas kernels, own_factor(): pl.pallas_call(functools.partial(factor_kernel, me), out_shape=(pltpu.VME...  1.48 us

profile of v3, /device:TPU:1, one launch (start us, length us, event | category | flops | bytes accessed | tf_op | source)
XLA Modules:
  0.0 51.7 jit_solution(1941648024879346157)
XLA Ops:
  0.6 1.5 %own_factor.1 = (bf16[4,16,512]{2,1,0:T(8,128)(2,1)S(1)}, f32[2,128]{1,0:T(2,128)S(1)}) custom-call(f32[2,8,2048]{2,1,0:T(8,128)} %shocks_ref.1, f32[1,8]{1,0:T(1,128)} %bitcast.13, s32[4,16]{1,0:T(4,128)} %bitcast.10, f32[4,16]{1,0:T(4,128)} %bitcast.11, s32[1,16]{1,0:T(1,128)} %bitcast.14, s32[1,16]{1,0:T(1,128)} %bitcast.15, f32[1,16]{1,0:T(1,128)} %bitcast.16, ...), custom_call_target="tpu_custom_call" | custom-call | tf_op jit(solution)/shard_map/own_factor/pallas_call | solution.py:131
  2.1 18.3 %gather_outer.1 = (bf16[16,4,16,512]{3,2,1,0:T(8,128)(2,1)S(1)}, bf16[32,256,256]{2,1,0:T(8,128)(2,1)S(1)}, f32[32,128,128]{2,1,0:T(8,128)S(1)}, f32[32,8,128]{2...) custom-call(bf16[4,16,512]{2,1,0:T(8,128)(2,1)S(1)} %get-tuple-eleme, ...), custom_call_target="tpu_custom_call" | custom-call | tf_op jit(solution)/shard_map/gather_outer/pallas_call | solution.py:403
  20.5 20.0 %revalue.1.slabs_ref = f32[8,24,128]{2,1,0:T(8,128)S(1)} custom-call(bf16[16,4,16,512]{3,2,1,0:T(8,128)(2,1)S(1)} %get-tuple-element.15.blocks_ref, bf16[32,256,256]{2,1,0:T(8,128)(2,1)S(1)} %get-tuple-element.16.weight_t, f32[32,128,128]{2,1,0:T(8,128)S(1)} %get-tuple-element.17.dwt, f32[32,8,128]{2,1,0:T(8,128)S(1)} %get-tuple-element.18.rows_t, ...), custom_call_target="tpu_custom_call" | custom-call | tf_op jit(solution)/shard_map/revalue/pallas_call | solution.py:558
  40.4 10.7 %scatter_inner.1.inbox_ref = f32[8,24,128]{2,1,0:T(8,128)S(1)} custom-call(f32[8,24,128]{2,1,0:T(8,128)S(1)} %revalue.1.slabs_ref), custom_call_target="tpu_custom_call" | custom-call | tf_op jit(solution)/shard_map/scatter_inner/pallas_call | solution.py:622
  51.1 0.6 %total_inner.1 = (f32[2,2,256]{2,1,0:T(2,128)}, f32[2,2,256]{2,1,0:T(2,128)}, f32[2,2,128]{2,1,0:T(2,128)}) custom-call(f32[8,24,128]{2,1,0:T(8,128)S(1)} %scatter_inner.1.inbox_ref), custom_call_target="tpu_custom_call" | custom-call | tf_op jit(solution)/shard_map/total_inner/pallas_call | solution.py:637

commit v4 on v3

--- a/solution.py
+++ b/solution.py
@@ -21,7 +21,8 @@
 GROUPS = 16
 TYPE, MAT, RATIO, FEE, MORT, ACC, SIG, KEY = 8, 9, 10, 11, 12, 13, 14, 15
 SLAB = 24
-MESSAGES = 50
+MESSAGES = 44
+UNROLL = 4
 LOG2E = 1.0 / math.log(2.0)
 UNIT = LOG2E / SMOOTH
 
@@ -55,7 +56,7 @@
     return lax.broadcasted_iota(jnp.int32, shape, dim)
 
 
-def factor_kernel(
+def own_factor(
     me,
     shocks_ref,
     sigma_ref,
@@ -71,7 +72,6 @@
     table_ref,
     scratch,
 ):
-    me = lax.axis_index("outer") if me is None else me
     sigma_row = sigma_ref[...]
     mat = mat_ref[...].astype(F32)
     number = (iota((1, 16), 1) + 16 * me).astype(F32)
@@ -127,19 +127,6 @@
         out_ref[g // 4, :, 128 * (g % 4) : 128 * (g % 4) + 128] = both.astype(BF16)
 
 
-def own_factor(shocks, sigma, index, alloc, *rest, me=None):
-    return pl.pallas_call(
-        functools.partial(factor_kernel, me),
-        out_shape=(
-            pltpu.VMEM((4, 16, 512), BF16),
-            pltpu.VMEM((2, 128), F32),
-        ),
-        scratch_shapes=[pltpu.VMEM((16, 128), F32)],
-        compiler_params=pltpu.CompilerParams(vmem_limit_bytes=8 << 20),
-        name="own_factor",
-    )(*in_hbm(shocks, sigma[None], index.T, alloc.T, *(value[None] for value in rest)))
-
-
 def spread():
     return (iota((16, 128), 1) % 16 == iota((16, 128), 0)).astype(F32)
 
@@ -257,8 +244,16 @@
 
 
 def gather_kernel(
-    block_ref,
-    table_ref,
+    shocks_ref,
+    sigma_ref,
+    index_ref,
+    alloc_ref,
+    kind_ref,
+    mat_ref,
+    ratio_ref,
+    fee_ref,
+    mort_ref,
+    account_ref,
     world_ref,
     rate_ref,
     blocks_ref,
@@ -269,6 +264,9 @@
     dates,
     plan_v,
     rank_ref,
+    block_ref,
+    table_ref,
+    scratch,
     tables_ref,
     table,
     level,
@@ -286,6 +284,23 @@
     barrier = pltpu.get_barrier_semaphore()
     for peer in peers:
         pl.semaphore_signal(barrier, inc=1, device_id={"outer": peer}, device_id_type=MESH)
+    own_factor(
+        me,
+        shocks_ref,
+        sigma_ref,
+        index_ref,
+        alloc_ref,
+        kind_ref,
+        mat_ref,
+        ratio_ref,
+        fee_ref,
+        mort_ref,
+        account_ref,
+        block_ref,
+        table_ref,
+        scratch,
+    )
+    date_tables(rate_ref, dates)
     pl.semaphore_wait(barrier, len(peers))
 
     started = []
@@ -329,25 +344,28 @@
     for color in range(2):
         q = 2 * color
         near.append([send_piece(shift(color, d, 0), me, q, 2, True) for d in (1, 3)])
+    far = [send_piece(shift(color, 2, 0), me, 2 * color, 2, True) for color in range(2)]
     home = []
     for color in range(2):
         q = 2 * color
         home.append([send_piece(shift(color, 0, d), me, q, 2, True) for d in (1, 3)])
 
-    date_tables(rate_ref, dates)
-
     second = []
-    far = []
     for side in range(2):
         for color in range(2):
             q = 2 * color
-            behind, onward = (3, 1) if side == 0 else (1, 3)
+            behind = 3 if side == 0 else 1
             near[color][side].wait_recv()
             origin = shift(color, behind, 0)
-            far.append((color, side, send_piece(shift(color, onward, 0), origin, q + side, 1)))
             for way, d in enumerate((1, 3)):
                 copy = send_piece(shift(color, 0, d), origin, q, 2)
                 second.append((color, behind, q, 2, way, copy))
+
+    for color in range(2):
+        far[color].wait_recv()
+        for way, d in enumerate((1, 3)):
+            copy = send_piece(shift(color, 0, d), shift(color, 2, 0), 2 * color, 2)
+            second.append((color, 2, 2 * color, 2, way, copy))
 
     last = []
 
@@ -368,19 +386,14 @@
     local[0].wait()
     line = tables_ref.at[pl.ds(row * 4, 4)]
     down = [post(next(numbers), at(d, 0), line, line) for d in (1, 3, 2)]
-    for color, side, copy in far:
-        copy.wait_recv()
-        for way, d in enumerate((1, 3)):
-            fresh = send_piece(shift(color, 0, d), shift(color, 2, 0), 2 * color + side, 1)
-            second.append((color, 2, 2 * color + side, 1, way, fresh))
     for copy in down:
         copy.wait_recv()
     params = cohort_order(tables_ref, table, plan_v, rank_ref)
     fund_levels(params, world_ref, level)
     for n, entry in enumerate(second):
         hand_on(*entry)
-        if n % 2 == 0:
-            build_tiles(2 * n, 4, table, level, weight_t, dwt, rows_t, acc_t)
+        if n < 8:
+            build_tiles(4 * n, 4, table, level, weight_t, dwt, rows_t, acc_t)
     for copy in last:
         copy.wait_recv()
     local[1].wait()
@@ -388,8 +401,9 @@
         copy.wait_send()
 
 
-def gather_outer(block, table, world, rate):
+def gather_outer(shocks, sigma, index, alloc, rows, world, rate):
     vmem = pl.BlockSpec(memory_space=pltpu.VMEM)
+    arguments = (shocks, sigma[None], index.T, alloc.T, *rows, world, rate.T)
     out_shape = (
         pltpu.VMEM((NOUT, 4, 16, 512), BF16),
         pltpu.VMEM((TILES, 256, 256), BF16),
@@ -403,9 +417,12 @@
     return pl.pallas_call(
         gather_kernel,
         out_shape=out_shape,
-        in_specs=[vmem] * 4,
+        in_specs=[vmem] * len(arguments),
         out_specs=(vmem,) * len(out_shape),
         scratch_shapes=[
+            pltpu.VMEM((4, 16, 512), BF16),
+            pltpu.VMEM((2, 128), F32),
+            pltpu.VMEM((16, 128), F32),
             pltpu.VMEM((NOUT, 2, 128), F32),
             pltpu.VMEM((2, 16, 128), F32),
             pltpu.VMEM((2, 128, 128), F32),
@@ -417,7 +434,7 @@
             collective_id=0, has_side_effects=True, vmem_limit_bytes=24 << 20
         ),
         name="gather_outer",
-    )(*in_vmem(block, table), *in_hbm(world, rate.T))
+    )(*in_hbm(*arguments))
 
 
 def value_kernel(
@@ -508,13 +525,13 @@
     raw(0, 0)
 
     def work(n, carry):
-        item_work(2 * n, 0)
-        item_work(2 * n + 1, 1)
+        for k in range(UNROLL):
+            item_work(UNROLL * n + k, k % 2)
         return carry
 
-    pairs = (plan[2, 0] + 1) // 2
-    lax.fori_loop(0, pairs, work, 0)
-    flush(2 * pairs - 1, 1)
+    rounds = (plan[2, 0] + (UNROLL - 1)) // UNROLL
+    lax.fori_loop(0, rounds, work, 0)
+    flush(UNROLL * rounds - 1, 1)
 
     def close(q, deltas):
         fresh = list(deltas)
@@ -662,19 +679,19 @@
     mortality,
     account,
 ):
-    block, table = own_factor(
-        inner_shocks,
-        fund_volatility,
-        fund_index,
-        allocation,
-        guarantee_type,
-        maturity,
-        guarantee_ratio,
-        fee_rate,
-        mortality,
-        account,
+    kinds = (guarantee_type, maturity, guarantee_ratio, fee_rate, mortality, account)
+    rows = [value[None] for value in kinds]
+    slabs = revalue(
+        *gather_outer(
+            inner_shocks,
+            fund_volatility,
+            fund_index,
+            allocation,
+            rows,
+            world_shocks,
+            short_rate,
+        )
     )
-    slabs = revalue(*gather_outer(block, table, world_shocks, short_rate))
     return scatter_inner(slabs)
 
 

time: 52.5 us -> 50.7 us (0.966); the launches traced: 51.7 us -> 50.6 us
  Pallas kernels: 51.1 us -> 49.9 us
    pallas_call x1, Pallas kernels: 20 us -> 19.2 us  [revalue(): pl.pallas_call(value_kernel, out_shape=pltpu.VMEM((NIN, SLAB, 128), F32),...]
    pallas_call x1, Pallas kernels: 10.7 us -> 10.1 us  [scatter_inner(): pl.pallas_call(scatter_kernel, out_shape=pltpu.VMEM((NIN, SLAB, 128), F32...]
    pallas_call x2 -> x1, Pallas kernels: 19.8 us -> 20 us  [gather_outer(): pl.pallas_call(gather_kernel, out_shape=out_shape, in_specs=[vmem] * len(...]
where the time goes in v4:
time: 50.7 us; the launch traced here: 50.6 us
  Pallas kernels  49.9 us (98%)
  between operations  0.66 us (1%)
    pallas_call x1, Pallas kernels, gather_outer(): pl.pallas_call(gather_kernel, out_shape=out_shape, in_specs=[vmem] * len(...  20 us
    pallas_call x1, Pallas kernels, revalue(): pl.pallas_call(value_kernel, out_shape=pltpu.VMEM((NIN, SLAB, 128), F32),...  19.2 us
    pallas_call x1, Pallas kernels, scatter_inner(): pl.pallas_call(scatter_kernel, out_shape=pltpu.VMEM((NIN, SLAB, 128), F32...  10.1 us

profile of v4, /device:TPU:1, one launch (start us, length us, event | category | flops | bytes accessed | tf_op | source)
XLA Modules:
  0.0 50.6 jit_solution(14609243183489791085)
XLA Ops:
  0.6 20.0 %gather_outer.1 = (bf16[16,4,16,512]{3,2,1,0:T(8,128)(2,1)S(1)}, bf16[32,256,256]{2,1,0:T(8,128)(2,1)S(1)}, f32[32,128,128]{2,1,0:T(8,128)S(1)}, f32[32,8,128]{2...) custom-call(f32[2,8,2048]{2,1,0:T(8,128)} %shocks_ref.1, ...), custom_call_target="tpu_custom_call" | custom-call | tf_op jit(solution)/shard_map/gather_outer/pallas_call | solution.py:417
  20.6 19.2 %revalue.1.slabs_ref = f32[8,24,128]{2,1,0:T(8,128)S(1)} custom-call(bf16[16,4,16,512]{3,2,1,0:T(8,128)(2,1)S(1)} %get-tuple-element.11.blocks_ref, bf16[32,256,256]{2,1,0:T(8,128)(2,1)S(1)} %get-tuple-element.12.weight_t, f32[32,128,128]{2,1,0:T(8,128)S(1)} %get-tuple-element.13.dwt, f32[32,8,128]{2,1,0:T(8,128)S(1)} %get-tuple-element.14.rows_t, ...), custom_call_target="tpu_custom_call" | custom-call | tf_op jit(solution)/shard_map/revalue/pallas_call | solution.py:575
  39.8 10.1 %scatter_inner.1.inbox_ref = f32[8,24,128]{2,1,0:T(8,128)S(1)} custom-call(f32[8,24,128]{2,1,0:T(8,128)S(1)} %revalue.1.slabs_ref), custom_call_target="tpu_custom_call" | custom-call | tf_op jit(solution)/shard_map/scatter_inner/pallas_call | solution.py:639
  49.9 0.6 %total_inner.1 = (f32[2,2,256]{2,1,0:T(2,128)}, f32[2,2,256]{2,1,0:T(2,128)}, f32[2,2,128]{2,1,0:T(2,128)}) custom-call(f32[8,24,128]{2,1,0:T(8,128)S(1)} %scatter_inner.1.inbox_ref), custom_call_target="tpu_custom_call" | custom-call | tf_op jit(solution)/shard_map/total_inner/pallas_call | solution.py:654

commit v5 on v4

--- a/solution.py
+++ b/solution.py
@@ -21,7 +21,7 @@
 GROUPS = 16
 TYPE, MAT, RATIO, FEE, MORT, ACC, SIG, KEY = 8, 9, 10, 11, 12, 13, 14, 15
 SLAB = 24
-MESSAGES = 44
+MESSAGES = 25
 UNROLL = 4
 LOG2E = 1.0 / math.log(2.0)
 UNIT = LOG2E / SMOOTH
@@ -303,30 +303,28 @@
     date_tables(rate_ref, dates)
     pl.semaphore_wait(barrier, len(peers))
 
-    started = []
-
-    def post(number, peer, src, dst):
+    def post(number, peer, src, dst, sent=0):
         copy = pltpu.make_async_remote_copy(
             src_ref=src,
             dst_ref=dst,
-            send_sem=send.at[number],
+            send_sem=send.at[sent],
             recv_sem=recv.at[number],
             device_id={"outer": peer},
             device_id_type=MESH,
         )
         copy.start()
-        started.append(copy)
         return copy
 
-    numbers = iter(range(MESSAGES))
-
-    def piece(origin, first, count):
-        return blocks_ref.at[origin, pl.ds(first, count)]
-
-    def send_piece(peer, origin, first, count, mine=False):
-        dst = piece(origin, first, count)
+    def whole(ref, count, semaphore):
+        view = ref.at[pl.ds(0, count)]
+        return pltpu.make_async_copy(view, view, semaphore)
+
+    numbers = iter(range(3, MESSAGES))
+
+    def send_piece(peer, origin, first, count, mine=False, number=None):
+        dst = blocks_ref.at[origin, pl.ds(first, count)]
         src = block_ref.at[pl.ds(first, count)] if mine else dst
-        return post(next(numbers), peer, src, dst)
+        return post(next(numbers) if number is None else number, peer, src, dst)
 
     local = [
         pltpu.make_async_copy(table_ref, tables_ref.at[me], own.at[0]),
@@ -335,7 +333,8 @@
     for copy in local:
         copy.start()
 
-    across = [post(next(numbers), at(0, d), table_ref, tables_ref.at[me]) for d in (1, 3, 2)]
+    for d in (1, 3, 2):
+        post(0, at(0, d), table_ref, tables_ref.at[me], 1)
 
     def shift(color, first_step, second_step):
         return at(second_step, first_step) if color == 0 else at(first_step, second_step)
@@ -350,55 +349,50 @@
         q = 2 * color
         home.append([send_piece(shift(color, 0, d), me, q, 2, True) for d in (1, 3)])
 
+    whole(tables_ref, 3, recv.at[0]).wait()
+    local[0].wait()
+    line = tables_ref.at[pl.ds(row * 4, 4)]
+    for d in (1, 3, 2):
+        post(1, at(d, 0), line, line, 1)
+
     second = []
+
+    def spread_second(color, offset):
+        for way, d in enumerate((1, 3)):
+            copy = send_piece(shift(color, 0, d), shift(color, offset, 0), 2 * color, 2)
+            second.append((color, offset, way, copy))
+
     for side in range(2):
         for color in range(2):
-            q = 2 * color
-            behind = 3 if side == 0 else 1
             near[color][side].wait_recv()
-            origin = shift(color, behind, 0)
-            for way, d in enumerate((1, 3)):
-                copy = send_piece(shift(color, 0, d), origin, q, 2)
-                second.append((color, behind, q, 2, way, copy))
+            spread_second(color, 3 if side == 0 else 1)
+
+    def hand_on(color, offset, way, copy):
+        copy.wait_recv()
+        behind, onward = (3, 1) if way == 0 else (1, 3)
+        origin = shift(color, offset, behind)
+        send_piece(shift(color, 0, onward), origin, 2 * color + way, 1, number=2)
 
     for color in range(2):
         far[color].wait_recv()
-        for way, d in enumerate((1, 3)):
-            copy = send_piece(shift(color, 0, d), shift(color, 2, 0), 2 * color, 2)
-            second.append((color, 2, 2 * color, 2, way, copy))
-
-    last = []
-
-    def hand_on(color, first, q, count, way, copy):
-        copy.wait_recv()
-        behind, onward = (3, 1) if way == 0 else (1, 3)
-        quarter = 2 * color + way
-        if not q <= quarter < q + count:
-            return
-        origin = shift(color, first, behind)
-        last.append(send_piece(shift(color, 0, onward), origin, quarter, 1))
-
+        spread_second(color, 2)
     for way in range(2):
         for color in range(2):
-            hand_on(color, 0, 2 * color, 2, way, home[color][way])
-    for copy in across:
-        copy.wait_recv()
-    local[0].wait()
-    line = tables_ref.at[pl.ds(row * 4, 4)]
-    down = [post(next(numbers), at(d, 0), line, line) for d in (1, 3, 2)]
-    for copy in down:
-        copy.wait_recv()
+            hand_on(color, 0, way, home[color][way])
+    whole(tables_ref, 12, recv.at[1]).wait()
     params = cohort_order(tables_ref, table, plan_v, rank_ref)
     fund_levels(params, world_ref, level)
+    tiles = 0
     for n, entry in enumerate(second):
+        more = (TILES * (n + 1) // 10) // 2 * 2 - tiles if n < 10 else 0
+        if more:
+            build_tiles(tiles, more, table, level, weight_t, dwt, rows_t, acc_t)
+            tiles += more
         hand_on(*entry)
-        if n < 8:
-            build_tiles(4 * n, 4, table, level, weight_t, dwt, rows_t, acc_t)
-    for copy in last:
-        copy.wait_recv()
+    whole(blocks_ref, 4, recv.at[2]).wait()
     local[1].wait()
-    for copy in started:
-        copy.wait_send()
+    whole(blocks_ref, 15, send.at[0]).wait()
+    whole(tables_ref, 15, send.at[1]).wait()
 
 
 def gather_outer(shocks, sigma, index, alloc, rows, world, rate):
@@ -426,7 +420,7 @@
             pltpu.VMEM((NOUT, 2, 128), F32),
             pltpu.VMEM((2, 16, 128), F32),
             pltpu.VMEM((2, 128, 128), F32),
-            pltpu.SemaphoreType.DMA((MESSAGES,)),
+            pltpu.SemaphoreType.DMA((2,)),
             pltpu.SemaphoreType.DMA((MESSAGES,)),
             pltpu.SemaphoreType.DMA((2,)),
         ],

time: 50.7 us -> 49 us (0.966)
  Pallas kernels: 49.9 us -> 47.8 us
    pallas_call x1, Pallas kernels: 20 us -> 17.3 us  [gather_outer(): pl.pallas_call(gather_kernel, out_shape=out_shape, in_specs=[vmem] * len(...]
    pallas_call x1, Pallas kernels: 10.1 us -> 10.7 us  [scatter_inner(): pl.pallas_call(scatter_kernel, out_shape=pltpu.VMEM((NIN, SLAB, 128), F32...]
where the time goes in v5:
time: 49 us; the launch traced here: 48.5 us
  Pallas kernels  47.8 us (98%)
  between operations  0.66 us (1%)
    pallas_call x1, Pallas kernels, revalue(): pl.pallas_call(value_kernel, out_shape=pltpu.VMEM((NIN, SLAB, 128), F32),...  19.2 us
    pallas_call x1, Pallas kernels, gather_outer(): pl.pallas_call(gather_kernel, out_shape=out_shape, in_specs=[vmem] * len(...  17.3 us
    pallas_call x1, Pallas kernels, scatter_inner(): pl.pallas_call(scatter_kernel, out_shape=pltpu.VMEM((NIN, SLAB, 128), F32...  10.7 us

profile of v5, /device:TPU:1, one launch (start us, length us, event | category | flops | bytes accessed | tf_op | source)
XLA Modules:
  0.0 48.5 jit_solution(17719404099991606759)
XLA Ops:
  0.6 17.3 %gather_outer.1 = (bf16[16,4,16,512]{3,2,1,0:T(8,128)(2,1)S(1)}, bf16[32,256,256]{2,1,0:T(8,128)(2,1)S(1)}, f32[32,128,128]{2,1,0:T(8,128)S(1)}, f32[32,8,128]{2...) custom-call(f32[2,8,2048]{2,1,0:T(8,128)} %shocks_ref.1, ...), custom_call_target="tpu_custom_call" | custom-call | tf_op jit(solution)/shard_map/gather_outer/pallas_call | solution.py:411
  17.9 19.2 %revalue.1.slabs_ref = f32[8,24,128]{2,1,0:T(8,128)S(1)} custom-call(bf16[16,4,16,512]{3,2,1,0:T(8,128)(2,1)S(1)} %get-tuple-element.11.blocks_ref, bf16[32,256,256]{2,1,0:T(8,128)(2,1)S(1)} %get-tuple-element.12.weight_t, f32[32,128,128]{2,1,0:T(8,128)S(1)} %get-tuple-element.13.dwt, f32[32,8,128]{2,1,0:T(8,128)S(1)} %get-tuple-element.14.rows_t, ...), custom_call_target="tpu_custom_call" | custom-call | tf_op jit(solution)/shard_map/revalue/pallas_call | solution.py:569
  37.1 10.7 %scatter_inner.1.inbox_ref = f32[8,24,128]{2,1,0:T(8,128)S(1)} custom-call(f32[8,24,128]{2,1,0:T(8,128)S(1)} %revalue.1.slabs_ref), custom_call_target="tpu_custom_call" | custom-call | tf_op jit(solution)/shard_map/scatter_inner/pallas_call | solution.py:633
  47.9 0.6 %total_inner.1 = (f32[2,2,256]{2,1,0:T(2,128)}, f32[2,2,256]{2,1,0:T(2,128)}, f32[2,2,128]{2,1,0:T(2,128)}) custom-call(f32[8,24,128]{2,1,0:T(8,128)S(1)} %scatter_inner.1.inbox_ref), custom_call_target="tpu_custom_call" | custom-call | tf_op jit(solution)/shard_map/total_inner/pallas_call | solution.py:648
